TPU v7x, 32 devices: a whole 2x2x4 slice. The times are simulated.
32 devices in a mesh: group: 2 (over core), trow: 2 (over y), tcol: 8 (over z, x).
Axes of the slice: x: 2, y: 2, z: 4, core: 2. Of those that a mesh axis runs over, the one named last changes fastest.
Arguments:
- displacement: float32 [3, 128, 64, 256], P(None, ('group', 'trow'), 'tcol'), may hold values from -6 to 6
- velocity: float32 [3, 128, 64, 256], P(None, ('group', 'trow'), 'tcol'), may hold values from -6 to 6
- stiffness: float32 [128, 64], P(('group', 'trow'), 'tcol'), may hold values from 4 to 12
- wet_position: float32 [3, 8192], P(None, ('group', 'trow', 'tcol')), may hold values from -6 to 6
- wet_normal: float32 [3, 8192], P(None, ('group', 'trow', 'tcol')), may hold values from -6 to 6
- wet_area: float32 [8192], P(('group', 'trow', 'tcol')), may hold values from 0.022097087 to 0.22097087
- wet_map: int32 [8192], P(('group', 'trow', 'tcol')), may hold values from 0 to 255
Outputs:
- displacement_out: float32 [3, 128, 64, 256], P(None, ('group', 'trow'), 'tcol')
- velocity_out: float32 [3, 128, 64, 256], P(None, ('group', 'trow'), 'tcol')
Inputs may be any that keep to these rules, and one draw needn't show every extreme that they name: Each wet point lies on the patch of nodes of the device that holds it: wet_map gives a * 8 + b for the node (a, b) of that patch.
All inputs are finite; a program needn't handle non-finite values.
Results may differ from a plain program's by a relative error of at most 0.0018.
Values may be sent and summed in bfloat16 or wider, within the bound.
A program may use at most 128 MiB of HBM per device.

v0:
```python
import math
import jax
import jax.numpy as jnp
from jax import lax
from jax.sharding import PartitionSpec as P

LOADS = 64
SUBSTEPS = 4
COUPLED = 2
WET_DEV = 256
SPHERE_AREA = 4.0 * math.pi
SMOOTHING = 0.1
TIME_STEP = 0.3
THICKNESS = 0.5
SPLINE_TAPS = (2.0 / 3.0, -1.0 / 12.0, -1.0 / 12.0, -1.0 / 6.0)


def padded_2(array, sides, width):
    for axis, dim in sides:
        count, length = (lax.axis_size(axis), array.shape[dim])
        up = [(i, (i + 1) % count) for i in range(count - 1)]
        down = [(j, i) for i, j in up]
        last = lax.slice_in_dim(array, length - width, length, axis=dim)
        first = lax.slice_in_dim(array, 0, width, axis=dim)
        before = lax.ppermute(last, axis, up)
        after = lax.ppermute(first, axis, down)
        array = jnp.concatenate([before, array, after], axis=dim)
    return array


def spline_apply(padded, height, breadth, margin):
    middle = padded[:, margin : margin + height, margin : margin + breadth]
    summed = 2.0 * SPLINE_TAPS[0] * middle
    for offset in (1, 2, 3):
        along_rows = (
            padded[:, margin + offset : margin + offset + height, margin : margin + breadth]
            + padded[:, margin - offset : margin - offset + height, margin : margin + breadth]
        )
        along_cols = (
            padded[:, margin : margin + height, margin + offset : margin + offset + breadth]
            + padded[:, margin : margin + height, margin - offset : margin - offset + breadth]
        )
        summed = summed + SPLINE_TAPS[offset] * (along_rows + along_cols)
    return summed


def thickness_term(values, stride):
    above_layer = jnp.concatenate([values[..., stride:], values[..., -stride:]], axis=3)
    below_layer = jnp.concatenate([values[..., :stride], values[..., :-stride]], axis=3)
    return 2.0 * values - above_layer - below_layer


def advance(displacement, velocity, stiffness_grid, loading, in_plane):
    acceleration = -(stiffness_grid * in_plane) - THICKNESS * thickness_term(displacement, LOADS)
    outermost = acceleration[..., -LOADS:] + loading
    acceleration = jnp.concatenate([acceleration[..., :-LOADS], outermost], axis=3)
    velocity = velocity + TIME_STEP * acceleration
    displacement = displacement + TIME_STEP * velocity
    return (displacement, velocity)


def kernel_tile(position, normal, area, targets):
    delta_x = targets[0][None, :] - position[0][:, None]
    delta_y = targets[1][None, :] - position[1][:, None]
    delta_z = targets[2][None, :] - position[2][:, None]
    numerator = (
        normal[0][:, None] * delta_x + normal[1][:, None] * delta_y + normal[2][:, None] * delta_z
    )
    squared = delta_x * delta_x + delta_y * delta_y + delta_z * delta_z + SMOOTHING * SMOOTHING
    weighted = area[:, None] * numerator
    return (weighted / (SPHERE_AREA * squared * jnp.sqrt(squared))).astype(jnp.bfloat16)


def normal_speeds(velocity, wet_normal, wet_map):
    outer_layer = velocity[..., -LOADS:]
    flattened = outer_layer.reshape(3, outer_layer.shape[1] * outer_layer.shape[2], LOADS)
    picked = jnp.take(flattened, wet_map, axis=1)
    speeds = (
        wet_normal[0][:, None] * picked[0]
        + wet_normal[1][:, None] * picked[1]
        + wet_normal[2][:, None] * picked[2]
    )
    return speeds.T


def node_loads(pressure, wet_normal, wet_map, height, breadth):
    node_count = height * breadth
    one_hot = (
        lax.broadcasted_iota(jnp.int32, (node_count, wet_map.shape[0]), 0) == wet_map[None, :]
    ).astype(jnp.float32)
    contribution = -(wet_normal[:, None, :] * pressure[None, :, :])
    loading = jnp.einsum("pw,kqw->kpq", one_hot, contribution, precision=lax.Precision.HIGHEST)
    return loading.reshape(3, height, breadth, LOADS)


def pressure_terms(sources, targets, gathered, block_size, block_count):
    position, normal, area = sources

    def accumulate(block_index, summed):
        tile = kernel_tile(
            position,
            normal,
            area,
            lax.dynamic_slice_in_dim(targets, block_index * block_size, block_size, 1),
        )
        partial_value = jnp.dot(gathered, tile, preferred_element_type=jnp.float32)
        return lax.dynamic_update_slice_in_dim(summed, partial_value, block_index * block_size, 1)

    initial = jnp.zeros((gathered.shape[0], block_size * block_count), jnp.float32)
    return lax.fori_loop(0, block_count, accumulate, initial)


def on_device(displacement, velocity, stiffness, wet_position, wet_normal, wet_area, wet_map):
    height = displacement.shape[1]
    breadth = displacement.shape[2]
    targets = lax.all_gather(wet_position, ("group", "trow"), axis=1, tiled=True)
    sources = (
        lax.all_gather(wet_position, "tcol", axis=1, tiled=True),
        lax.all_gather(wet_normal, "tcol", axis=1, tiled=True),
        lax.all_gather(wet_area, "tcol", axis=0, tiled=True),
    )
    target_count = targets.shape[1]
    factor = 2
    block_size = WET_DEV * factor
    block_count = target_count // block_size
    stiffness_grid = stiffness[None, :, :, None]
    for repeat in range(COUPLED):
        speeds = normal_speeds(velocity, wet_normal, wet_map)
        speed_rounded = speeds.astype(jnp.bfloat16)
        gathered = lax.all_gather(speed_rounded, "tcol", axis=1, tiled=True)
        partial_value = pressure_terms(sources, targets, gathered, block_size, block_count)
        received = lax.psum_scatter(
            partial_value, ("group", "trow"), scatter_dimension=1, tiled=True
        )
        pressure = 0.5 * speeds + received
        loading = node_loads(pressure, wet_normal, wet_map, height, breadth)
        for substep in range(SUBSTEPS):
            padded = padded_2(displacement, ((("group", "trow"), 1), ("tcol", 2)), 3)
            in_plane = spline_apply(padded, height, breadth, 3)
            displacement, velocity = advance(
                displacement, velocity, stiffness_grid, loading, in_plane
            )
    return (displacement, velocity)


def solution(mesh):
    placed = (
        P(None, ("group", "trow"), "tcol", None),
        P(None, ("group", "trow"), "tcol", None),
        P(("group", "trow"), "tcol"),
        P(None, ("group", "trow", "tcol")),
        P(None, ("group", "trow", "tcol")),
        P(("group", "trow", "tcol")),
        P(("group", "trow", "tcol")),
    )
    return jax.shard_map(
        on_device,
        mesh=mesh,
        in_specs=placed,
        out_specs=(
            P(None, ("group", "trow"), "tcol", None),
            P(None, ("group", "trow"), "tcol", None),
        ),
        check_vma=False,
    )
```

profile of v0, /device:TPU:0, one launch (start us, length us, event | category | flops | bytes accessed | tf_op | source)
XLA Modules:
  0.0 489.0 jit_solution(4813544611088728946)
XLA Ops:
  8.1 4.9 %collective-permute-start.1 = (f32[3,3,8,256]{3,2,1,0:T(8,128)S(1)}, f32[3,3,8,256]{3,2,1,0:T(8,128)S(1)}, u32[]{:S(2)}, u32[]{:S(2)}) collective-permute-start(f32[3,3,8,256]{3,2,1,0:T(8,128)S(1)} %get-tuple-element.425), channel_id=1, source_target_pairs={{0,8},{8,16},{16,24},{1,9},{9,17},{17,25},{2,10},{10,18},{18,26},{... | collective-permute-start | bytes 221192 | tf_op jit(solution)/shard_map/ppermute | solution.py:25
  16.6 31.1 %all_gather.19 = f32[3,2048]{1,0:T(4,128)S(1)} all-gather(f32[3,256]{1,0:T(4,128)} %param.17), channel_id=1, replica_groups=mesh['group'=2,'trow'=2,'tcol'=8] {'tcol'}, dimensions={1}, use_global_device_ids=true | all-gather | bytes 27648 | tf_op jit(solution)/shard_map/all_gather | solution.py:119
  47.6 30.7 %all_gather.21 = f32[3,2048]{1,0:T(4,128)S(1)} all-gather(f32[3,256]{1,0:T(4,128)} %param.16), channel_id=1, replica_groups=mesh['group'=2,'trow'=2,'tcol'=8] {'tcol'}, dimensions={1}, use_global_device_ids=true | all-gather | bytes 27648 | tf_op jit(solution)/shard_map/all_gather | solution.py:118
  78.4 12.3 %all_gather.20 = f32[3,1024]{1,0:T(4,128)} all-gather(f32[3,256]{1,0:T(4,128)} %param.16), channel_id=1, replica_groups=mesh['group'=2,'trow'=2,'tcol'=8] {'group','trow'}, dimensions={1}, use_global_device_ids=true | all-gather | bytes 15360 | tf_op jit(solution)/shard_map/all_gather | solution.py:116
  94.0 31.3 %all_gather.22 = bf16[64,2048]{0,1:T(8,128)(2,1)S(1)} all-gather(bf16[64,256]{0,1:T(8,128)(2,1)S(1)} %get-tuple-element.319), channel_id=1, replica_groups=mesh['group'=2,'trow'=2,'tcol'=8] {'tcol'}, dimensions={1}, use_global_device_ids=true | all-gather | bytes 294912 | tf_op jit(solution)/shard_map/all_gather | solution.py:130
  125.4 20.6 %all-gather = f32[8,1,256]{2,1,0:T(1,128)S(1)} all-gather(f32[1,1,256]{2,1,0:T(1,128)S(1)} %bitcast.189), channel_id=1, replica_groups=mesh['group'=2,'trow'=2,'tcol'=8] {'tcol'}, dimensions={0}, use_global_device_ids=true | all-gather | bytes 9216 | tf_op jit(solution)/shard_map/all_gather | solution.py:120
  146.1 11.3 %while.26 = (s32[]{:T(128)}, f32[64,1024]{1,0:T(8,128)S(1)}, f32[2048]{0:T(1024)S(1)}, f32[3,2048]{1,0:T(4,128)S(1)}, f32[3,1024]{1,0:T(4,128)}, /*index=5*/f32[...) while((s32[]{:T(128)}, f32[64,1024]{1,0:T(8,128)S(1)}, ...), condition=%wide.region_1.3_spmd, body=%wide.region_0.0_spmd.sunk | while | flops 154140672 | bytes 567507 | solution.py:110
  147.0 4.7 fusion.287
  152.7 4.7 fusion.287
  162.3 5.4 %collective-permute-start.3 = (f32[3,38,3,256]{3,2,1,0:T(4,128)}, f32[3,38,3,256]{3,2,1,0:T(4,128)}, u32[]{:S(2)}, u32[]{:S(2)}) collective-permute-start(f32[3,38,3,256]{3,2,1,0:T(4,128)} %get-tuple-element.374), channel_id=1, source_target_pairs={{0,1},{1,2},{2,3},{3,4},{4,5},{5,6},{6,7},{8,9},{9,10},{10,11},{11... | collective-permute-start | bytes 1050632 | tf_op jit(solution)/shard_map/ppermute | solution.py:25
  167.6 1.4 fusion.270
  169.3 2.4 collective-permute-done.2
  171.6 1.6 collective-permute-done.3
  173.2 5.7 %fusion.156 = f32[3,32,8,256]{3,2,1,0:T(8,128)S(1)} fusion(f32[3,38,8,256]{3,2,1,0:T(8,128)} %copy-done.5, f32[3,38,3,256]{3,2,1,0:T(4,128)} %collective-permute-done.3, f32[3,38,3,256]{3,2,1,0:T(4,128)} %copy-done.16, f32[3,35,8,256]{3,2,1,0:T(8,128)} %copy-done.3, f32[3,35,8,256]{3,2,1,0:T(8,128)S(1)} %get-tuple-element.429, ...), kind=kLoop, calls=%fused_computation.249 | loop fusion | flops 6094848 | bytes 9499648 | tf_op jit(solution)/shard_map/sub | solution.py:54
  182.3 4.5 collective-permute-start.5
  187.3 1.6 collective-permute-done.5
  190.4 5.2 %collective-permute-start.7 = (f32[3,38,3,256]{3,2,1,0:T(4,128)S(1)}, f32[3,38,3,256]{3,2,1,0:T(4,128)S(1)}, u32[]{:S(2)}, u32[]{:S(2)}) collective-permute-start(f32[3,38,3,256]{3,2,1,0:T(4,128)S(1)} %get-tuple-element.372), channel_id=1, source_target_pairs={{0,1},{1,2},{2,3},{3,4},{4,5},{5,6},{6,7},{8,9},{9,10},{10,11},{11... | collective-permute-start | bytes 1050632 | tf_op jit(solution)/shard_map/ppermute | solution.py:25
  196.1 8.9 %collective-permute-done.6 = f32[3,38,3,256]{3,2,1,0:T(4,128)S(1)} collective-permute-done((f32[3,38,3,256]{3,2,1,0:T(4,128)S(1)}, f32[3,38,3,256]{3,2,1,0:T(4,128)S(1)}, u32[]{:S(2)}, u32[]{:S(2)}) %collective-permute-start.6) | collective-permute-done | bytes 350240 | tf_op jit(solution)/shard_map/ppermute | solution.py:26
  204.9 10.2 %collective-permute-done.7 = f32[3,38,3,256]{3,2,1,0:T(4,128)S(1)} collective-permute-done((f32[3,38,3,256]{3,2,1,0:T(4,128)S(1)}, f32[3,38,3,256]{3,2,1,0:T(4,128)S(1)}, u32[]{:S(2)}, u32[]{:S(2)}) %collective-permute-start.7) | collective-permute-done | bytes 350240 | tf_op jit(solution)/shard_map/ppermute | solution.py:25
  215.6 1.6 fusion.140
  217.9 1.3 collective-permute-start.8
  219.2 4.5 collective-permute-start.9
  224.1 1.6 collective-permute-done.9
  225.9 1.3 collective-permute-start.10
  227.2 5.0 %collective-permute-start.11 = (f32[3,38,3,256]{3,2,1,0:T(4,128)S(1)}, f32[3,38,3,256]{3,2,1,0:T(4,128)S(1)}, u32[]{:S(2)}, u32[]{:S(2)}) collective-permute-start(f32[3,38,3,256]{3,2,1,0:T(4,128)S(1)} %get-tuple-element.368), channel_id=1, source_target_pairs={{0,1},{1,2},{2,3},{3,4},{4,5},{5,6},{6,7},{8,9},{9,10},{10,11},{11... | collective-permute-start | bytes 1050632 | tf_op jit(solution)/shard_map/ppermute | solution.py:25
  232.7 8.6 %collective-permute-done.10 = f32[3,38,3,256]{3,2,1,0:T(4,128)S(1)} collective-permute-done((f32[3,38,3,256]{3,2,1,0:T(4,128)S(1)}, f32[3,38,3,256]{3,2,1,0:T(4,128)S(1)}, u32[]{:S(2)}, u32[]{:S(2)}) %collective-permute-start.10) | collective-permute-done | bytes 350240 | tf_op jit(solution)/shard_map/ppermute | solution.py:26
  241.3 10.2 %collective-permute-done.11 = f32[3,38,3,256]{3,2,1,0:T(4,128)S(1)} collective-permute-done((f32[3,38,3,256]{3,2,1,0:T(4,128)S(1)}, f32[3,38,3,256]{3,2,1,0:T(4,128)S(1)}, u32[]{:S(2)}, u32[]{:S(2)}) %collective-permute-start.11) | collective-permute-done | bytes 350240 | tf_op jit(solution)/shard_map/ppermute | solution.py:25
  252.0 1.6 fusion.124
  255.4 4.5 collective-permute-start.13
  260.3 1.6 collective-permute-done.13
  263.8 5.0 %collective-permute-start.15 = (f32[3,38,3,256]{3,2,1,0:T(4,128)S(1)}, f32[3,38,3,256]{3,2,1,0:T(4,128)S(1)}, u32[]{:S(2)}, u32[]{:S(2)}) collective-permute-start(f32[3,38,3,256]{3,2,1,0:T(4,128)S(1)} %get-tuple-element.364), channel_id=1, source_target_pairs={{0,1},{1,2},{2,3},{3,4},{4,5},{5,6},{6,7},{8,9},{9,10},{10,11},{11... | collective-permute-start | bytes 1050632 | tf_op jit(solution)/shard_map/ppermute | solution.py:25
  269.3 9.1 %collective-permute-done.14 = f32[3,38,3,256]{3,2,1,0:T(4,128)S(1)} collective-permute-done((f32[3,38,3,256]{3,2,1,0:T(4,128)S(1)}, f32[3,38,3,256]{3,2,1,0:T(4,128)S(1)}, u32[]{:S(2)}, u32[]{:S(2)}) %collective-permute-start.14) | collective-permute-done | bytes 350240 | tf_op jit(solution)/shard_map/ppermute | solution.py:26
  278.4 10.3 %collective-permute-done.15 = f32[3,38,3,256]{3,2,1,0:T(4,128)S(1)} collective-permute-done((f32[3,38,3,256]{3,2,1,0:T(4,128)S(1)}, f32[3,38,3,256]{3,2,1,0:T(4,128)S(1)}, u32[]{:S(2)}, u32[]{:S(2)}) %collective-permute-start.15) | collective-permute-done | bytes 350240 | tf_op jit(solution)/shard_map/ppermute | solution.py:25
  289.2 1.6 fusion.108
  293.9 31.5 %all_gather.23 = bf16[64,2048]{0,1:T(8,128)(2,1)S(1)} all-gather(bf16[64,256]{0,1:T(8,128)(2,1)S(1)} %get-tuple-element.313), channel_id=1, replica_groups=mesh['group'=2,'trow'=2,'tcol'=8] {'tcol'}, dimensions={1}, use_global_device_ids=true | all-gather | bytes 294912 | tf_op jit(solution)/shard_map/all_gather | solution.py:130
  327.0 4.8 collective-permute-start.17
  331.8 11.3 %while.27 = (s32[]{:T(128)}, f32[64,1024]{1,0:T(8,128)S(1)}, f32[2048]{0:T(1024)S(1)}, f32[3,2048]{1,0:T(4,128)S(1)}, f32[3,1024]{1,0:T(4,128)}, /*index=5*/f32[...) while((s32[]{:T(128)}, f32[64,1024]{1,0:T(8,128)S(1)}, ...), condition=%wide.region_4.6_spmd, body=%wide.region_3.5_spmd.sunk | while | flops 154140672 | bytes 567507 | solution.py:110
  332.8 4.7 fusion.291
  338.4 4.7 fusion.291
  345.4 5.3 %collective-permute-start.19 = (f32[3,38,3,256]{3,2,1,0:T(4,128)S(1)}, f32[3,38,3,256]{3,2,1,0:T(4,128)}, u32[]{:S(2)}, u32[]{:S(2)}) collective-permute-start(f32[3,38,3,256]{3,2,1,0:T(4,128)S(1)} %get-tuple-element.360), channel_id=1, source_target_pairs={{0,1},{1,2},{2,3},{3,4},{4,5},{5,6},{6,7},{8,9},{9,10},{10,11},{11... | collective-permute-start | bytes 1050632 | tf_op jit(solution)/shard_map/ppermute | solution.py:25
  352.2 4.9 collective-permute-done.18
  357.1 8.0 %collective-permute-done.19 = f32[3,38,3,256]{3,2,1,0:T(4,128)} collective-permute-done((f32[3,38,3,256]{3,2,1,0:T(4,128)S(1)}, f32[3,38,3,256]{3,2,1,0:T(4,128)}, u32[]{:S(2)}, u32[]{:S(2)}) %collective-permute-start.19) | collective-permute-done | bytes 350240 | tf_op jit(solution)/shard_map/ppermute | solution.py:25
  365.1 1.7 pad_maximum_fusion.3
  366.8 2.6 fusion.92
  373.4 4.5 collective-permute-start.21
  378.3 1.6 collective-permute-done.21
  380.2 1.3 collective-permute-start.22
  381.5 4.6 collective-permute-start.23
  386.5 8.5 %collective-permute-done.22 = f32[3,38,3,256]{3,2,1,0:T(4,128)S(1)} collective-permute-done((f32[3,38,3,256]{3,2,1,0:T(4,128)S(1)}, f32[3,38,3,256]{3,2,1,0:T(4,128)S(1)}, u32[]{:S(2)}, u32[]{:S(2)}) %collective-permute-start.22) | collective-permute-done | bytes 350240 | tf_op jit(solution)/shard_map/ppermute | solution.py:26
  395.0 10.2 %collective-permute-done.23 = f32[3,38,3,256]{3,2,1,0:T(4,128)S(1)} collective-permute-done((f32[3,38,3,256]{3,2,1,0:T(4,128)S(1)}, f32[3,38,3,256]{3,2,1,0:T(4,128)S(1)}, u32[]{:S(2)}, u32[]{:S(2)}) %collective-permute-start.23) | collective-permute-done | bytes 350240 | tf_op jit(solution)/shard_map/ppermute | solution.py:25
  405.7 1.6 fusion.76
  409.2 4.5 collective-permute-start.25
  414.1 1.6 collective-permute-done.25
  417.2 5.3 %collective-permute-start.27 = (f32[3,38,3,256]{3,2,1,0:T(4,128)S(1)}, f32[3,38,3,256]{3,2,1,0:T(4,128)S(1)}, u32[]{:S(2)}, u32[]{:S(2)}) collective-permute-start(f32[3,38,3,256]{3,2,1,0:T(4,128)S(1)} %get-tuple-element.352), channel_id=1, source_target_pairs={{0,1},{1,2},{2,3},{3,4},{4,5},{5,6},{6,7},{8,9},{9,10},{10,11},{11... | collective-permute-start | bytes 1050632 | tf_op jit(solution)/shard_map/ppermute | solution.py:25
  423.0 8.8 %collective-permute-done.26 = f32[3,38,3,256]{3,2,1,0:T(4,128)S(1)} collective-permute-done((f32[3,38,3,256]{3,2,1,0:T(4,128)S(1)}, f32[3,38,3,256]{3,2,1,0:T(4,128)S(1)}, u32[]{:S(2)}, u32[]{:S(2)}) %collective-permute-start.26) | collective-permute-done | bytes 350240 | tf_op jit(solution)/shard_map/ppermute | solution.py:26
  431.8 10.2 %collective-permute-done.27 = f32[3,38,3,256]{3,2,1,0:T(4,128)S(1)} collective-permute-done((f32[3,38,3,256]{3,2,1,0:T(4,128)S(1)}, f32[3,38,3,256]{3,2,1,0:T(4,128)S(1)}, u32[]{:S(2)}, u32[]{:S(2)}) %collective-permute-start.27) | collective-permute-done | bytes 350240 | tf_op jit(solution)/shard_map/ppermute | solution.py:25
  442.5 1.6 fusion.60
  445.9 4.5 collective-permute-start.29
  450.9 1.6 collective-permute-done.29
  454.0 5.0 %collective-permute-start.31 = (f32[3,38,3,256]{3,2,1,0:T(4,128)S(1)}, f32[3,38,3,256]{3,2,1,0:T(4,128)S(1)}, u32[]{:S(2)}, u32[]{:S(2)}) collective-permute-start(f32[3,38,3,256]{3,2,1,0:T(4,128)S(1)} %get-tuple-element.348), channel_id=1, source_target_pairs={{0,1},{1,2},{2,3},{3,4},{4,5},{5,6},{6,7},{8,9},{9,10},{10,11},{11... | collective-permute-start | bytes 1050632 | tf_op jit(solution)/shard_map/ppermute | solution.py:25
  459.5 8.6 %collective-permute-done.30 = f32[3,38,3,256]{3,2,1,0:T(4,128)S(1)} collective-permute-done((f32[3,38,3,256]{3,2,1,0:T(4,128)S(1)}, f32[3,38,3,256]{3,2,1,0:T(4,128)S(1)}, u32[]{:S(2)}, u32[]{:S(2)}) %collective-permute-start.30) | collective-permute-done | bytes 350240 | tf_op jit(solution)/shard_map/ppermute | solution.py:26
  468.1 10.2 %collective-permute-done.31 = f32[3,38,3,256]{3,2,1,0:T(4,128)S(1)} collective-permute-done((f32[3,38,3,256]{3,2,1,0:T(4,128)S(1)}, f32[3,38,3,256]{3,2,1,0:T(4,128)S(1)}, u32[]{:S(2)}, u32[]{:S(2)}) %collective-permute-start.31) | collective-permute-done | bytes 350240 | tf_op jit(solution)/shard_map/ppermute | solution.py:25
  478.8 1.6 fusion.44
  480.7 1.5 multiply_add_fusion
  (197 shorter events, 53.1 us)
Async XLA Ops:
  7.2 171.8 %reduce-scatter.3.cloned.1.call-start = ((), (), s32[]{:S(2)}) async-start(), calls=%async_computation.2 | async-start | bytes 655360 | tf_op jit(solution)/shard_map/reduce_scatter | solution.py:132
  8.1 150.4 %collective-permute-start.1 = (f32[3,3,8,256]{3,2,1,0:T(8,128)S(1)}, f32[3,3,8,256]{3,2,1,0:T(8,128)S(1)}, u32[]{:S(2)}, u32[]{:S(2)}) collective-permute-start(f32[3,3,8,256]{3,2,1,0:T(8,128)S(1)} %get-tuple-element.425), channel_id=1, source_target_pairs={{0,8},{8,16},{16,24},{1,9},{9,17},{17,25},{2,10},{10,18},{18,26},{... | collective-permute-start | bytes 221192 | tf_op jit(solution)/shard_map/ppermute | solution.py:25
  13.1 145.8 %collective-permute-start = (f32[3,3,8,256]{3,2,1,0:T(8,128)S(1)}, f32[3,3,8,256]{3,2,1,0:T(8,128)S(1)}, u32[]{:S(2)}, u32[]{:S(2)}) collective-permute-start(f32[3,3,8,256]{3,2,1,0:T(8,128)S(1)} %get-tuple-element.424), channel_id=1, source_target_pairs={{8,0},{16,8},{24,16},{9,1},{17,9},{25,17},{10,2},{18,10},{26,18},{... | collective-permute-start | bytes 221192 | tf_op jit(solution)/shard_map/ppermute | solution.py:26
  15.7 78.0 %copy-start.31 = (pred[256]{0:T(512)(128)(4,1)}, pred[256]{0:T(512)(128)(4,1)S(1)}, u32[]{:S(2)}) copy-start(pred[256]{0:T(512)(128)(4,1)S(1)} %compare_and_fusion) | copy-start | bytes 772
  16.5 77.2 %copy-start.21 = (f32[1,256]{1,0:T(1,128)}, f32[1,256]{1,0:T(1,128)S(1)}, u32[]{:S(2)}) copy-start(f32[1,256]{1,0:T(1,128)S(1)} %get-tuple-element.433) | copy-start | bytes 3076
  16.5 77.2 %copy-start.23 = (f32[1,256]{1,0:T(1,128)}, f32[1,256]{1,0:T(1,128)S(1)}, u32[]{:S(2)}) copy-start(f32[1,256]{1,0:T(1,128)S(1)} %get-tuple-element.434) | copy-start | bytes 3076
  16.5 77.2 %copy-start.25 = (f32[1,256]{1,0:T(1,128)}, f32[1,256]{1,0:T(1,128)S(1)}, u32[]{:S(2)}) copy-start(f32[1,256]{1,0:T(1,128)S(1)} %get-tuple-element.435) | copy-start | bytes 3076
  90.7 3.1 copy-start.27
  93.1 32.3 %copy-start.33 = (f32[256]{0:T(256)S(1)}, f32[256]{0:T(256)}, u32[]{:S(2)}) copy-start(f32[256]{0:T(256)} %param.18) | copy-start | bytes 3076
  157.4 1.4 copy-start.6
  157.4 1.4 copy-start.8
  158.5 211.7 %reduce-scatter.5.cloned.1.call-start = ((), (), s32[]{:S(2)}) async-start(), calls=%async_computation.3 | async-start | bytes 655360 | tf_op jit(solution)/shard_map/reduce_scatter | solution.py:132
  159.7 9.3 %copy-start.5 = (f32[3,38,8,256]{3,2,1,0:T(8,128)}, f32[3,38,8,256]{3,2,1,0:T(8,128)S(1)}, u32[]{:S(2)}) copy-start(f32[3,38,8,256]{3,2,1,0:T(8,128)S(1)} %get-tuple-element.430) | copy-start | bytes 2801668
  161.0 10.7 %collective-permute-start.2 = (f32[3,38,3,256]{3,2,1,0:T(4,128)}, f32[3,38,3,256]{3,2,1,0:T(4,128)S(1)}, u32[]{:S(2)}, u32[]{:S(2)}) collective-permute-start(f32[3,38,3,256]{3,2,1,0:T(4,128)} %get-tuple-element.373), channel_id=1, source_target_pairs={{1,0},{2,1},{3,2},{4,3},{5,4},{6,5},{7,6},{9,8},{10,9},{11,10},{12... | collective-permute-start | bytes 1050632 | tf_op jit(solution)/shard_map/ppermute | solution.py:26
  162.3 6.9 %copy-start.30 = (f32[32,8]{0,1:T(8,128)S(1)}, f32[32,8]{0,1:T(8,128)}, u32[]{:S(2)}) copy-start(f32[32,8]{0,1:T(8,128)} %param.15) | copy-start | bytes 3076
  162.3 10.9 %collective-permute-start.3 = (f32[3,38,3,256]{3,2,1,0:T(4,128)}, f32[3,38,3,256]{3,2,1,0:T(4,128)}, u32[]{:S(2)}, u32[]{:S(2)}) collective-permute-start(f32[3,38,3,256]{3,2,1,0:T(4,128)} %get-tuple-element.374), channel_id=1, source_target_pairs={{0,1},{1,2},{2,3},{3,4},{4,5},{5,6},{6,7},{8,9},{9,10},{10,11},{11... | collective-permute-start | bytes 1050632 | tf_op jit(solution)/shard_map/ppermute | solution.py:25
  171.6 1.6 copy-start.16
  173.2 6.9 %copy-start.17 = (f32[3,256]{1,0:T(4,128)S(1)}, f32[3,256]{1,0:T(4,128)}, u32[]{:S(2)}) copy-start(f32[3,256]{1,0:T(4,128)} %param.17) | copy-start | bytes 9220
  173.2 6.9 %copy-start.19 = (s32[256]{0:T(256)S(1)}, s32[256]{0:T(256)}, u32[]{:S(2)}) copy-start(s32[256]{0:T(256)} %param.19) | copy-start | bytes 3076
  178.9 1.8 copy-start.4
  181.0 6.2 %collective-permute-start.4 = (f32[3,3,8,256]{3,2,1,0:T(8,128)S(1)}, f32[3,3,8,256]{3,2,1,0:T(8,128)S(1)}, u32[]{:S(2)}, u32[]{:S(2)}) collective-permute-start(f32[3,3,8,256]{3,2,1,0:T(8,128)S(1)} %get-tuple-element.415), channel_id=1, source_target_pairs={{8,0},{16,8},{24,16},{9,1},{17,9},{25,17},{10,2},{18,10},{26,18},{... | collective-permute-start | bytes 221192 | tf_op jit(solution)/shard_map/ppermute | solution.py:26
  182.3 6.5 %collective-permute-start.5 = (f32[3,3,8,256]{3,2,1,0:T(8,128)S(1)}, f32[3,3,8,256]{3,2,1,0:T(8,128)S(1)}, u32[]{:S(2)}, u32[]{:S(2)}) collective-permute-start(f32[3,3,8,256]{3,2,1,0:T(8,128)S(1)} %get-tuple-element.416), channel_id=1, source_target_pairs={{0,8},{8,16},{16,24},{1,9},{9,17},{17,25},{2,10},{10,18},{18,26},{... | collective-permute-start | bytes 221192 | tf_op jit(solution)/shard_map/ppermute | solution.py:25
  189.1 15.8 %collective-permute-start.6 = (f32[3,38,3,256]{3,2,1,0:T(4,128)S(1)}, f32[3,38,3,256]{3,2,1,0:T(4,128)S(1)}, u32[]{:S(2)}, u32[]{:S(2)}) collective-permute-start(f32[3,38,3,256]{3,2,1,0:T(4,128)S(1)} %get-tuple-element.371), channel_id=1, source_target_pairs={{1,0},{2,1},{3,2},{4,3},{5,4},{6,5},{7,6},{9,8},{10,9},{11,10},{12... | collective-permute-start | bytes 1050632 | tf_op jit(solution)/shard_map/ppermute | solution.py:26
  190.4 24.7 %collective-permute-start.7 = (f32[3,38,3,256]{3,2,1,0:T(4,128)S(1)}, f32[3,38,3,256]{3,2,1,0:T(4,128)S(1)}, u32[]{:S(2)}, u32[]{:S(2)}) collective-permute-start(f32[3,38,3,256]{3,2,1,0:T(4,128)S(1)} %get-tuple-element.372), channel_id=1, source_target_pairs={{0,1},{1,2},{2,3},{3,4},{4,5},{5,6},{6,7},{8,9},{9,10},{10,11},{11... | collective-permute-start | bytes 1050632 | tf_op jit(solution)/shard_map/ppermute | solution.py:25
  217.8 35.9 %copy-start.1 = (f32[3,32,8,256]{3,2,1,0:T(8,128)}, f32[3,32,8,256]{3,2,1,0:T(8,128)S(1)}, u32[]{:S(2)}) copy-start(f32[3,32,8,256]{3,2,1,0:T(8,128)S(1)} %get-tuple-element.318) | copy-start | bytes 2359300
  217.9 6.2 %collective-permute-start.8 = (f32[3,3,8,256]{3,2,1,0:T(8,128)S(1)}, f32[3,3,8,256]{3,2,1,0:T(8,128)S(1)}, u32[]{:S(2)}, u32[]{:S(2)}) collective-permute-start(f32[3,3,8,256]{3,2,1,0:T(8,128)S(1)} %get-tuple-element.409), channel_id=1, source_target_pairs={{8,0},{16,8},{24,16},{9,1},{17,9},{25,17},{10,2},{18,10},{26,18},{... | collective-permute-start | bytes 221192 | tf_op jit(solution)/shard_map/ppermute | solution.py:26
  219.2 6.5 %collective-permute-start.9 = (f32[3,3,8,256]{3,2,1,0:T(8,128)S(1)}, f32[3,3,8,256]{3,2,1,0:T(8,128)S(1)}, u32[]{:S(2)}, u32[]{:S(2)}) collective-permute-start(f32[3,3,8,256]{3,2,1,0:T(8,128)S(1)} %get-tuple-element.410), channel_id=1, source_target_pairs={{0,8},{8,16},{16,24},{1,9},{9,17},{17,25},{2,10},{10,18},{18,26},{... | collective-permute-start | bytes 221192 | tf_op jit(solution)/shard_map/ppermute | solution.py:25
  225.9 15.4 %collective-permute-start.10 = (f32[3,38,3,256]{3,2,1,0:T(4,128)S(1)}, f32[3,38,3,256]{3,2,1,0:T(4,128)S(1)}, u32[]{:S(2)}, u32[]{:S(2)}) collective-permute-start(f32[3,38,3,256]{3,2,1,0:T(4,128)S(1)} %get-tuple-element.367), channel_id=1, source_target_pairs={{1,0},{2,1},{3,2},{4,3},{5,4},{6,5},{7,6},{9,8},{10,9},{11,10},{12... | collective-permute-start | bytes 1050632 | tf_op jit(solution)/shard_map/ppermute | solution.py:26
  227.2 24.3 %collective-permute-start.11 = (f32[3,38,3,256]{3,2,1,0:T(4,128)S(1)}, f32[3,38,3,256]{3,2,1,0:T(4,128)S(1)}, u32[]{:S(2)}, u32[]{:S(2)}) collective-permute-start(f32[3,38,3,256]{3,2,1,0:T(4,128)S(1)} %get-tuple-element.368), channel_id=1, source_target_pairs={{0,1},{1,2},{2,3},{3,4},{4,5},{5,6},{6,7},{8,9},{9,10},{10,11},{11... | collective-permute-start | bytes 1050632 | tf_op jit(solution)/shard_map/ppermute | solution.py:25
  254.1 6.2 %collective-permute-start.12 = (f32[3,3,8,256]{3,2,1,0:T(8,128)S(1)}, f32[3,3,8,256]{3,2,1,0:T(8,128)S(1)}, u32[]{:S(2)}, u32[]{:S(2)}) collective-permute-start(f32[3,3,8,256]{3,2,1,0:T(8,128)S(1)} %get-tuple-element.403), channel_id=1, source_target_pairs={{8,0},{16,8},{24,16},{9,1},{17,9},{25,17},{10,2},{18,10},{26,18},{... | collective-permute-start | bytes 221192 | tf_op jit(solution)/shard_map/ppermute | solution.py:26
  255.4 6.5 %collective-permute-start.13 = (f32[3,3,8,256]{3,2,1,0:T(8,128)S(1)}, f32[3,3,8,256]{3,2,1,0:T(8,128)S(1)}, u32[]{:S(2)}, u32[]{:S(2)}) collective-permute-start(f32[3,3,8,256]{3,2,1,0:T(8,128)S(1)} %get-tuple-element.404), channel_id=1, source_target_pairs={{0,8},{8,16},{16,24},{1,9},{9,17},{17,25},{2,10},{10,18},{18,26},{... | collective-permute-start | bytes 221192 | tf_op jit(solution)/shard_map/ppermute | solution.py:25
  260.3 1.8 copy-start.11
  262.5 15.9 %collective-permute-start.14 = (f32[3,38,3,256]{3,2,1,0:T(4,128)S(1)}, f32[3,38,3,256]{3,2,1,0:T(4,128)S(1)}, u32[]{:S(2)}, u32[]{:S(2)}) collective-permute-start(f32[3,38,3,256]{3,2,1,0:T(4,128)S(1)} %get-tuple-element.363), channel_id=1, source_target_pairs={{1,0},{2,1},{3,2},{4,3},{5,4},{6,5},{7,6},{9,8},{10,9},{11,10},{12... | collective-permute-start | bytes 1050632 | tf_op jit(solution)/shard_map/ppermute | solution.py:26
  263.8 24.8 %collective-permute-start.15 = (f32[3,38,3,256]{3,2,1,0:T(4,128)S(1)}, f32[3,38,3,256]{3,2,1,0:T(4,128)S(1)}, u32[]{:S(2)}, u32[]{:S(2)}) collective-permute-start(f32[3,38,3,256]{3,2,1,0:T(4,128)S(1)} %get-tuple-element.364), channel_id=1, source_target_pairs={{0,1},{1,2},{2,3},{3,4},{4,5},{5,6},{6,7},{8,9},{9,10},{10,11},{11... | collective-permute-start | bytes 1050632 | tf_op jit(solution)/shard_map/ppermute | solution.py:25
  269.0 19.6 %copy-start.12 = (f32[3,3,8,256]{3,2,1,0:T(8,128)S(1)}, f32[3,3,8,256]{3,2,1,0:T(8,128)}, u32[]{:S(2)}) copy-start(f32[3,3,8,256]{3,2,1,0:T(8,128)} %copy-done.11) | copy-start | bytes 221188
  269.0 19.6 %copy-start.14 = (f32[3,3,8,256]{3,2,1,0:T(8,128)S(1)}, f32[3,3,8,256]{3,2,1,0:T(8,128)}, u32[]{:S(2)}) copy-start(f32[3,3,8,256]{3,2,1,0:T(8,128)} %copy-done.13) | copy-start | bytes 221188
  289.2 1.8 copy-start.2
  291.3 1.6 copy-start.32
  291.3 1.8 copy-start.22
  291.3 1.8 copy-start.24
  291.3 1.8 copy-start.26
  292.9 38.8 %copy-start.7 = (f32[3,2048]{1,0:T(4,128)S(1)}, f32[3,2048]{1,0:T(4,128)}, u32[]{:S(2)}) copy-start(f32[3,2048]{1,0:T(4,128)} %copy-done.6) | copy-start | bytes 73732
  293.0 38.8 %copy-start.9 = (f32[3,2048]{1,0:T(4,128)S(1)}, f32[3,2048]{1,0:T(4,128)}, u32[]{:S(2)}) copy-start(f32[3,2048]{1,0:T(4,128)} %copy-done.8) | copy-start | bytes 73732
  293.0 38.8 %copy-start.29 = (f32[2048]{0:T(1024)S(1)}, f32[2048]{0:T(1024)}, u32[]{:S(2)}) copy-start(f32[2048]{0:T(1024)} %copy-done.28) | copy-start | bytes 24580
  325.7 17.5 %collective-permute-start.16 = (f32[3,3,8,256]{3,2,1,0:T(8,128)S(1)}, f32[3,3,8,256]{3,2,1,0:T(8,128)S(1)}, u32[]{:S(2)}, u32[]{:S(2)}) collective-permute-start(f32[3,3,8,256]{3,2,1,0:T(8,128)S(1)} %get-tuple-element.397), channel_id=1, source_target_pairs={{8,0},{16,8},{24,16},{9,1},{17,9},{25,17},{10,2},{18,10},{26,18},{... | collective-permute-start | bytes 221192 | tf_op jit(solution)/shard_map/ppermute | solution.py:26
  327.0 16.2 %collective-permute-start.17 = (f32[3,3,8,256]{3,2,1,0:T(8,128)S(1)}, f32[3,3,8,256]{3,2,1,0:T(8,128)S(1)}, u32[]{:S(2)}, u32[]{:S(2)}) collective-permute-start(f32[3,3,8,256]{3,2,1,0:T(8,128)S(1)} %get-tuple-element.398), channel_id=1, source_target_pairs={{0,8},{8,16},{16,24},{1,9},{9,17},{17,25},{2,10},{10,18},{18,26},{... | collective-permute-start | bytes 221192 | tf_op jit(solution)/shard_map/ppermute | solution.py:25
  343.1 22.0 %copy-start.10 = (f32[3,3,8,256]{3,2,1,0:T(8,128)}, f32[3,3,8,256]{3,2,1,0:T(8,128)S(1)}, u32[]{:S(2)}) copy-start(f32[3,3,8,256]{3,2,1,0:T(8,128)S(1)} %collective-permute-done.17) | copy-start | bytes 221188
  344.1 13.0 %collective-permute-start.18 = (f32[3,38,3,256]{3,2,1,0:T(4,128)}, f32[3,38,3,256]{3,2,1,0:T(4,128)}, u32[]{:S(2)}, u32[]{:S(2)}) collective-permute-start(f32[3,38,3,256]{3,2,1,0:T(4,128)} %get-tuple-element.359), channel_id=1, source_target_pairs={{1,0},{2,1},{3,2},{4,3},{5,4},{6,5},{7,6},{9,8},{10,9},{11,10},{12... | collective-permute-start | bytes 1050632 | tf_op jit(solution)/shard_map/ppermute | solution.py:26
  345.4 19.7 %collective-permute-start.19 = (f32[3,38,3,256]{3,2,1,0:T(4,128)S(1)}, f32[3,38,3,256]{3,2,1,0:T(4,128)}, u32[]{:S(2)}, u32[]{:S(2)}) collective-permute-start(f32[3,38,3,256]{3,2,1,0:T(4,128)S(1)} %get-tuple-element.360), channel_id=1, source_target_pairs={{0,1},{1,2},{2,3},{3,4},{4,5},{5,6},{6,7},{8,9},{9,10},{10,11},{11... | collective-permute-start | bytes 1050632 | tf_op jit(solution)/shard_map/ppermute | solution.py:25
  366.8 3.3 copy-start.15
  366.8 4.3 copy-start.18
  366.8 4.3 copy-start.20
  372.1 6.2 %collective-permute-start.20 = (f32[3,3,8,256]{3,2,1,0:T(8,128)S(1)}, f32[3,3,8,256]{3,2,1,0:T(8,128)S(1)}, u32[]{:S(2)}, u32[]{:S(2)}) collective-permute-start(f32[3,3,8,256]{3,2,1,0:T(8,128)S(1)} %get-tuple-element.391), channel_id=1, source_target_pairs={{8,0},{16,8},{24,16},{9,1},{17,9},{25,17},{10,2},{18,10},{26,18},{... | collective-permute-start | bytes 221192 | tf_op jit(solution)/shard_map/ppermute | solution.py:26
  373.4 6.5 %collective-permute-start.21 = (f32[3,3,8,256]{3,2,1,0:T(8,128)S(1)}, f32[3,3,8,256]{3,2,1,0:T(8,128)S(1)}, u32[]{:S(2)}, u32[]{:S(2)}) collective-permute-start(f32[3,3,8,256]{3,2,1,0:T(8,128)S(1)} %get-tuple-element.392), channel_id=1, source_target_pairs={{0,8},{8,16},{16,24},{1,9},{9,17},{17,25},{2,10},{10,18},{18,26},{... | collective-permute-start | bytes 221192 | tf_op jit(solution)/shard_map/ppermute | solution.py:25
  380.2 14.8 %collective-permute-start.22 = (f32[3,38,3,256]{3,2,1,0:T(4,128)S(1)}, f32[3,38,3,256]{3,2,1,0:T(4,128)S(1)}, u32[]{:S(2)}, u32[]{:S(2)}) collective-permute-start(f32[3,38,3,256]{3,2,1,0:T(4,128)S(1)} %get-tuple-element.355), channel_id=1, source_target_pairs={{1,0},{2,1},{3,2},{4,3},{5,4},{6,5},{7,6},{9,8},{10,9},{11,10},{12... | collective-permute-start | bytes 1050632 | tf_op jit(solution)/shard_map/ppermute | solution.py:26
  381.5 23.7 %collective-permute-start.23 = (f32[3,38,3,256]{3,2,1,0:T(4,128)S(1)}, f32[3,38,3,256]{3,2,1,0:T(4,128)S(1)}, u32[]{:S(2)}, u32[]{:S(2)}) collective-permute-start(f32[3,38,3,256]{3,2,1,0:T(4,128)S(1)} %get-tuple-element.356), channel_id=1, source_target_pairs={{0,1},{1,2},{2,3},{3,4},{4,5},{5,6},{6,7},{8,9},{9,10},{10,11},{11... | collective-permute-start | bytes 1050632 | tf_op jit(solution)/shard_map/ppermute | solution.py:25
  407.9 6.2 %collective-permute-start.24 = (f32[3,3,8,256]{3,2,1,0:T(8,128)S(1)}, f32[3,3,8,256]{3,2,1,0:T(8,128)S(1)}, u32[]{:S(2)}, u32[]{:S(2)}) collective-permute-start(f32[3,3,8,256]{3,2,1,0:T(8,128)S(1)} %get-tuple-element.385), channel_id=1, source_target_pairs={{8,0},{16,8},{24,16},{9,1},{17,9},{25,17},{10,2},{18,10},{26,18},{... | collective-permute-start | bytes 221192 | tf_op jit(solution)/shard_map/ppermute | solution.py:26
  409.2 6.5 %collective-permute-start.25 = (f32[3,3,8,256]{3,2,1,0:T(8,128)S(1)}, f32[3,3,8,256]{3,2,1,0:T(8,128)S(1)}, u32[]{:S(2)}, u32[]{:S(2)}) collective-permute-start(f32[3,3,8,256]{3,2,1,0:T(8,128)S(1)} %get-tuple-element.386), channel_id=1, source_target_pairs={{0,8},{8,16},{16,24},{1,9},{9,17},{17,25},{2,10},{10,18},{18,26},{... | collective-permute-start | bytes 221192 | tf_op jit(solution)/shard_map/ppermute | solution.py:25
  415.9 15.9 %collective-permute-start.26 = (f32[3,38,3,256]{3,2,1,0:T(4,128)S(1)}, f32[3,38,3,256]{3,2,1,0:T(4,128)S(1)}, u32[]{:S(2)}, u32[]{:S(2)}) collective-permute-start(f32[3,38,3,256]{3,2,1,0:T(4,128)S(1)} %get-tuple-element.351), channel_id=1, source_target_pairs={{1,0},{2,1},{3,2},{4,3},{5,4},{6,5},{7,6},{9,8},{10,9},{11,10},{12... | collective-permute-start | bytes 1050632 | tf_op jit(solution)/shard_map/ppermute | solution.py:26
  417.2 24.8 %collective-permute-start.27 = (f32[3,38,3,256]{3,2,1,0:T(4,128)S(1)}, f32[3,38,3,256]{3,2,1,0:T(4,128)S(1)}, u32[]{:S(2)}, u32[]{:S(2)}) collective-permute-start(f32[3,38,3,256]{3,2,1,0:T(4,128)S(1)} %get-tuple-element.352), channel_id=1, source_target_pairs={{0,1},{1,2},{2,3},{3,4},{4,5},{5,6},{6,7},{8,9},{9,10},{10,11},{11... | collective-permute-start | bytes 1050632 | tf_op jit(solution)/shard_map/ppermute | solution.py:25
  444.6 6.2 %collective-permute-start.28 = (f32[3,3,8,256]{3,2,1,0:T(8,128)S(1)}, f32[3,3,8,256]{3,2,1,0:T(8,128)S(1)}, u32[]{:S(2)}, u32[]{:S(2)}) collective-permute-start(f32[3,3,8,256]{3,2,1,0:T(8,128)S(1)} %get-tuple-element.379), channel_id=1, source_target_pairs={{8,0},{16,8},{24,16},{9,1},{17,9},{25,17},{10,2},{18,10},{26,18},{... | collective-permute-start | bytes 221192 | tf_op jit(solution)/shard_map/ppermute | solution.py:26
  445.9 6.5 %collective-permute-start.29 = (f32[3,3,8,256]{3,2,1,0:T(8,128)S(1)}, f32[3,3,8,256]{3,2,1,0:T(8,128)S(1)}, u32[]{:S(2)}, u32[]{:S(2)}) collective-permute-start(f32[3,3,8,256]{3,2,1,0:T(8,128)S(1)} %get-tuple-element.380), channel_id=1, source_target_pairs={{0,8},{8,16},{16,24},{1,9},{9,17},{17,25},{2,10},{10,18},{18,26},{... | collective-permute-start | bytes 221192 | tf_op jit(solution)/shard_map/ppermute | solution.py:25
  452.7 15.4 %collective-permute-start.30 = (f32[3,38,3,256]{3,2,1,0:T(4,128)S(1)}, f32[3,38,3,256]{3,2,1,0:T(4,128)S(1)}, u32[]{:S(2)}, u32[]{:S(2)}) collective-permute-start(f32[3,38,3,256]{3,2,1,0:T(4,128)S(1)} %get-tuple-element.347), channel_id=1, source_target_pairs={{1,0},{2,1},{3,2},{4,3},{5,4},{6,5},{7,6},{9,8},{10,9},{11,10},{12... | collective-permute-start | bytes 1050632 | tf_op jit(solution)/shard_map/ppermute | solution.py:26
  454.0 24.3 %collective-permute-start.31 = (f32[3,38,3,256]{3,2,1,0:T(4,128)S(1)}, f32[3,38,3,256]{3,2,1,0:T(4,128)S(1)}, u32[]{:S(2)}, u32[]{:S(2)}) collective-permute-start(f32[3,38,3,256]{3,2,1,0:T(4,128)S(1)} %get-tuple-element.348), channel_id=1, source_target_pairs={{0,1},{1,2},{2,3},{3,4},{4,5},{5,6},{6,7},{8,9},{9,10},{10,11},{11... | collective-permute-start | bytes 1050632 | tf_op jit(solution)/shard_map/ppermute | solution.py:25
  (4 other events, 4.1 us)
Sparse Core Ops, SparseCore 0:
  158.6 18.0 reduce-scatter.2
  352.1 18.0 reduce-scatter.4
where the time goes:
time: 491 us; the launch traced here: 489 us
  blocking collectives  157 us (32%)
  waiting for transfers between devices  143 us (29%)
  starting transfers between devices  98.5 us (20%)
  other arithmetic  33 us (7%)
  local copies, waits for them, and re-layouts  22.1 us (5%)
  matrix products  19.5 us (4%)
  between operations  15.3 us (3%)
    ppermute x16, waiting for transfers between devices, padded_2(): before = lax.ppermute(last, axis, up)  80.1 us
    ppermute x16, starting transfers between devices, padded_2(): before = lax.ppermute(last, axis, up)  77.8 us
    all_gather x2, blocking collectives, on_device(): gathered = lax.all_gather(speed_rounded, 'tcol', axis=1, tiled=True)  62.8 us
    ppermute x16, waiting for transfers between devices, padded_2(): after = lax.ppermute(first, axis, down)  62.1 us
    all_gather x1, blocking collectives, on_device(): lax.all_gather(wet_normal, 'tcol', axis=1, tiled=True)  31.1 us
    all_gather x1, blocking collectives, on_device(): lax.all_gather(wet_position, 'tcol', axis=1, tiled=True)  30.7 us
    ppermute x16, starting transfers between devices, padded_2(): after = lax.ppermute(first, axis, down)  20.6 us
    all_gather x1, blocking collectives, on_device(): lax.all_gather(wet_area, 'tcol', axis=0, tiled=True)  20.6 us
  transfers between devices with their start and end apart: 34, of which 29 were waited for; matrix products, arithmetic and copies ran while one was open for 9% of the time, Pallas kernels for 0%

commit v1 on v0

--- a/solution.py
+++ b/solution.py
@@ -127,7 +127,8 @@
     for repeat in range(COUPLED):
         speeds = normal_speeds(velocity, wet_normal, wet_map)
         speed_rounded = speeds.astype(jnp.bfloat16)
-        gathered = lax.all_gather(speed_rounded, "tcol", axis=1, tiled=True)
+        blocks = lax.all_gather(speed_rounded, "tcol")
+        gathered = jnp.concatenate(blocks, axis=1)
         partial_value = pressure_terms(sources, targets, gathered, block_size, block_count)
         received = lax.psum_scatter(
             partial_value, ("group", "trow"), scatter_dimension=1, tiled=True

time: 491 us -> 490 us (level)
  no operation moved by 1% of the time
where the time goes in v1:
time: 490 us; the launch traced here: 488 us
  blocking collectives  156 us (32%)
  waiting for transfers between devices  143 us (29%)
  starting transfers between devices  98.8 us (20%)
  other arithmetic  33 us (7%)
  local copies, waits for them, and re-layouts  22.1 us (5%)
  matrix products  19.5 us (4%)
  between operations  15.3 us (3%)
    ppermute x16, waiting for transfers between devices, padded_2(): before = lax.ppermute(last, axis, up)  80.3 us
    ppermute x16, starting transfers between devices, padded_2(): before = lax.ppermute(last, axis, up)  78.1 us
    ppermute x16, waiting for transfers between devices, padded_2(): after = lax.ppermute(first, axis, down)  62.4 us
    all_gather x2, blocking collectives, on_device(): blocks = lax.all_gather(speed_rounded, 'tcol')  61.5 us
    all_gather x1, blocking collectives, on_device(): lax.all_gather(wet_normal, 'tcol', axis=1, tiled=True)  31.1 us
    all_gather x1, blocking collectives, on_device(): lax.all_gather(wet_position, 'tcol', axis=1, tiled=True)  30.7 us
    ppermute x16, starting transfers between devices, padded_2(): after = lax.ppermute(first, axis, down)  20.6 us
    all_gather x1, blocking collectives, on_device(): lax.all_gather(wet_area, 'tcol', axis=0, tiled=True)  20.5 us
  transfers between devices with their start and end apart: 34, of which 29 were waited for; matrix products, arithmetic and copies ran while one was open for 9% of the time, Pallas kernels for 0%

profile of v1, /device:TPU:0, one launch (start us, length us, event | category | flops | bytes accessed | tf_op | source)
XLA Modules:
  0.0 488.0 jit_solution(6184426121161419390)
XLA Ops:
  8.1 4.9 %collective-permute-start.1 = (f32[3,3,8,256]{3,2,1,0:T(8,128)S(1)}, f32[3,3,8,256]{3,2,1,0:T(8,128)S(1)}, u32[]{:S(2)}, u32[]{:S(2)}) collective-permute-start(f32[3,3,8,256]{3,2,1,0:T(8,128)S(1)} %get-tuple-element.397), channel_id=1, source_target_pairs={{0,8},{8,16},{16,24},{1,9},{9,17},{17,25},{2,10},{10,18},{18,26},{... | collective-permute-start | bytes 221192 | tf_op jit(solution)/shard_map/ppermute | solution.py:25
  16.6 31.1 %all_gather.25 = f32[3,2048]{1,0:T(4,128)S(1)} all-gather(f32[3,256]{1,0:T(4,128)} %param.17), channel_id=1, replica_groups=mesh['group'=2,'trow'=2,'tcol'=8] {'tcol'}, dimensions={1}, use_global_device_ids=true | all-gather | bytes 27648 | tf_op jit(solution)/shard_map/all_gather | solution.py:119
  47.6 30.7 %all_gather.27 = f32[3,2048]{1,0:T(4,128)S(1)} all-gather(f32[3,256]{1,0:T(4,128)} %param.16), channel_id=1, replica_groups=mesh['group'=2,'trow'=2,'tcol'=8] {'tcol'}, dimensions={1}, use_global_device_ids=true | all-gather | bytes 27648 | tf_op jit(solution)/shard_map/all_gather | solution.py:118
  78.4 12.3 %all_gather.26 = f32[3,1024]{1,0:T(4,128)} all-gather(f32[3,256]{1,0:T(4,128)} %param.16), channel_id=1, replica_groups=mesh['group'=2,'trow'=2,'tcol'=8] {'group','trow'}, dimensions={1}, use_global_device_ids=true | all-gather | bytes 15360 | tf_op jit(solution)/shard_map/all_gather | solution.py:116
  94.1 30.7 %all-gather = bf16[512,256]{1,0:T(8,128)(2,1)S(1)} all-gather(bf16[64,256]{1,0:T(8,128)(2,1)S(1)} %copy.68), channel_id=2, replica_groups=mesh['group'=2,'trow'=2,'tcol'=8] {'tcol'}, dimensions={0}, use_global_device_ids=true | all-gather | bytes 294912 | tf_op jit(solution)/shard_map/all_gather | solution.py:130
  124.8 20.5 %all-gather.2 = f32[8,1,256]{2,1,0:T(1,128)S(1)} all-gather(f32[1,1,256]{2,1,0:T(1,128)S(1)} %bitcast.203), channel_id=1, replica_groups=mesh['group'=2,'trow'=2,'tcol'=8] {'tcol'}, dimensions={0}, use_global_device_ids=true | all-gather | bytes 9216 | tf_op jit(solution)/shard_map/all_gather | solution.py:120
  145.4 11.3 %while.26 = (s32[]{:T(128)}, f32[64,1024]{1,0:T(8,128)S(1)}, f32[2048]{0:T(1024)S(1)}, f32[3,2048]{1,0:T(4,128)S(1)}, f32[3,1024]{1,0:T(4,128)}, /*index=5*/f32[...) while((s32[]{:T(128)}, f32[64,1024]{1,0:T(8,128)S(1)}, ...), condition=%wide.region_1.3_spmd, body=%wide.region_0.0_spmd.sunk | while | flops 154140672 | bytes 567507 | solution.py:110
  146.3 4.7 fusion.287
  152.0 4.7 fusion.287
  161.6 5.4 %collective-permute-start.3 = (f32[3,38,3,256]{3,2,1,0:T(4,128)}, f32[3,38,3,256]{3,2,1,0:T(4,128)}, u32[]{:S(2)}, u32[]{:S(2)}) collective-permute-start(f32[3,38,3,256]{3,2,1,0:T(4,128)} %get-tuple-element.346), channel_id=1, source_target_pairs={{0,1},{1,2},{2,3},{3,4},{4,5},{5,6},{6,7},{8,9},{9,10},{10,11},{11... | collective-permute-start | bytes 1050632 | tf_op jit(solution)/shard_map/ppermute | solution.py:25
  166.9 1.4 fusion.270
  168.6 2.4 collective-permute-done.2
  170.9 1.6 collective-permute-done.3
  172.5 5.7 %fusion.156 = f32[3,32,8,256]{3,2,1,0:T(8,128)S(1)} fusion(f32[3,38,8,256]{3,2,1,0:T(8,128)} %copy-done.5, f32[3,38,3,256]{3,2,1,0:T(4,128)} %collective-permute-done.3, f32[3,38,3,256]{3,2,1,0:T(4,128)} %copy-done.16, f32[3,35,8,256]{3,2,1,0:T(8,128)} %copy-done.3, f32[3,35,8,256]{3,2,1,0:T(8,128)S(1)} %get-tuple-element.401, ...), kind=kLoop, calls=%fused_computation.249 | loop fusion | flops 6094848 | bytes 9499648 | tf_op jit(solution)/shard_map/sub | solution.py:54
  180.3 1.3 collective-permute-start.4
  181.6 4.5 collective-permute-start.5
  186.6 1.6 collective-permute-done.5
  188.4 1.3 collective-permute-start.6
  189.7 5.2 %collective-permute-start.7 = (f32[3,38,3,256]{3,2,1,0:T(4,128)S(1)}, f32[3,38,3,256]{3,2,1,0:T(4,128)S(1)}, u32[]{:S(2)}, u32[]{:S(2)}) collective-permute-start(f32[3,38,3,256]{3,2,1,0:T(4,128)S(1)} %get-tuple-element.344), channel_id=1, source_target_pairs={{0,1},{1,2},{2,3},{3,4},{4,5},{5,6},{6,7},{8,9},{9,10},{10,11},{11... | collective-permute-start | bytes 1050632 | tf_op jit(solution)/shard_map/ppermute | solution.py:25
  195.4 8.8 %collective-permute-done.6 = f32[3,38,3,256]{3,2,1,0:T(4,128)S(1)} collective-permute-done((f32[3,38,3,256]{3,2,1,0:T(4,128)S(1)}, f32[3,38,3,256]{3,2,1,0:T(4,128)S(1)}, u32[]{:S(2)}, u32[]{:S(2)}) %collective-permute-start.6) | collective-permute-done | bytes 350240 | tf_op jit(solution)/shard_map/ppermute | solution.py:26
  204.2 10.2 %collective-permute-done.7 = f32[3,38,3,256]{3,2,1,0:T(4,128)S(1)} collective-permute-done((f32[3,38,3,256]{3,2,1,0:T(4,128)S(1)}, f32[3,38,3,256]{3,2,1,0:T(4,128)S(1)}, u32[]{:S(2)}, u32[]{:S(2)}) %collective-permute-start.7) | collective-permute-done | bytes 350240 | tf_op jit(solution)/shard_map/ppermute | solution.py:25
  214.9 1.6 fusion.140
  218.5 4.5 collective-permute-start.9
  223.4 1.6 collective-permute-done.9
  226.5 5.0 %collective-permute-start.11 = (f32[3,38,3,256]{3,2,1,0:T(4,128)S(1)}, f32[3,38,3,256]{3,2,1,0:T(4,128)S(1)}, u32[]{:S(2)}, u32[]{:S(2)}) collective-permute-start(f32[3,38,3,256]{3,2,1,0:T(4,128)S(1)} %get-tuple-element.340), channel_id=1, source_target_pairs={{0,1},{1,2},{2,3},{3,4},{4,5},{5,6},{6,7},{8,9},{9,10},{10,11},{11... | collective-permute-start | bytes 1050632 | tf_op jit(solution)/shard_map/ppermute | solution.py:25
  232.0 8.6 %collective-permute-done.10 = f32[3,38,3,256]{3,2,1,0:T(4,128)S(1)} collective-permute-done((f32[3,38,3,256]{3,2,1,0:T(4,128)S(1)}, f32[3,38,3,256]{3,2,1,0:T(4,128)S(1)}, u32[]{:S(2)}, u32[]{:S(2)}) %collective-permute-start.10) | collective-permute-done | bytes 350240 | tf_op jit(solution)/shard_map/ppermute | solution.py:26
  240.6 10.2 %collective-permute-done.11 = f32[3,38,3,256]{3,2,1,0:T(4,128)S(1)} collective-permute-done((f32[3,38,3,256]{3,2,1,0:T(4,128)S(1)}, f32[3,38,3,256]{3,2,1,0:T(4,128)S(1)}, u32[]{:S(2)}, u32[]{:S(2)}) %collective-permute-start.11) | collective-permute-done | bytes 350240 | tf_op jit(solution)/shard_map/ppermute | solution.py:25
  251.3 1.6 fusion.124
  254.6 4.5 collective-permute-start.13
  259.6 1.6 collective-permute-done.13
  263.1 5.0 %collective-permute-start.15 = (f32[3,38,3,256]{3,2,1,0:T(4,128)S(1)}, f32[3,38,3,256]{3,2,1,0:T(4,128)S(1)}, u32[]{:S(2)}, u32[]{:S(2)}) collective-permute-start(f32[3,38,3,256]{3,2,1,0:T(4,128)S(1)} %get-tuple-element.336), channel_id=1, source_target_pairs={{0,1},{1,2},{2,3},{3,4},{4,5},{5,6},{6,7},{8,9},{9,10},{10,11},{11... | collective-permute-start | bytes 1050632 | tf_op jit(solution)/shard_map/ppermute | solution.py:25
  268.6 9.1 %collective-permute-done.14 = f32[3,38,3,256]{3,2,1,0:T(4,128)S(1)} collective-permute-done((f32[3,38,3,256]{3,2,1,0:T(4,128)S(1)}, f32[3,38,3,256]{3,2,1,0:T(4,128)S(1)}, u32[]{:S(2)}, u32[]{:S(2)}) %collective-permute-start.14) | collective-permute-done | bytes 350240 | tf_op jit(solution)/shard_map/ppermute | solution.py:26
  277.7 10.2 %collective-permute-done.15 = f32[3,38,3,256]{3,2,1,0:T(4,128)S(1)} collective-permute-done((f32[3,38,3,256]{3,2,1,0:T(4,128)S(1)}, f32[3,38,3,256]{3,2,1,0:T(4,128)S(1)}, u32[]{:S(2)}, u32[]{:S(2)}) %collective-permute-start.15) | collective-permute-done | bytes 350240 | tf_op jit(solution)/shard_map/ppermute | solution.py:25
  288.5 1.6 fusion.108
  293.5 30.8 %all-gather.1 = bf16[512,256]{1,0:T(8,128)(2,1)S(1)} all-gather(bf16[64,256]{1,0:T(8,128)(2,1)S(1)} %copy.75), channel_id=3, replica_groups=mesh['group'=2,'trow'=2,'tcol'=8] {'tcol'}, dimensions={0}, use_global_device_ids=true | all-gather | bytes 294912 | tf_op jit(solution)/shard_map/all_gather | solution.py:130
  325.5 4.8 collective-permute-start.17
  330.4 11.3 %while.27 = (s32[]{:T(128)}, f32[64,1024]{1,0:T(8,128)S(1)}, f32[2048]{0:T(1024)S(1)}, f32[3,2048]{1,0:T(4,128)S(1)}, f32[3,1024]{1,0:T(4,128)}, /*index=5*/f32[...) while((s32[]{:T(128)}, f32[64,1024]{1,0:T(8,128)S(1)}, ...), condition=%wide.region_4.6_spmd, body=%wide.region_3.5_spmd.sunk | while | flops 154140672 | bytes 567507 | solution.py:110
  331.3 4.7 fusion.291
  337.0 4.7 fusion.291
  344.0 5.3 %collective-permute-start.19 = (f32[3,38,3,256]{3,2,1,0:T(4,128)S(1)}, f32[3,38,3,256]{3,2,1,0:T(4,128)}, u32[]{:S(2)}, u32[]{:S(2)}) collective-permute-start(f32[3,38,3,256]{3,2,1,0:T(4,128)S(1)} %get-tuple-element.332), channel_id=1, source_target_pairs={{0,1},{1,2},{2,3},{3,4},{4,5},{5,6},{6,7},{8,9},{9,10},{10,11},{11... | collective-permute-start | bytes 1050632 | tf_op jit(solution)/shard_map/ppermute | solution.py:25
  350.8 5.0 %collective-permute-done.18 = f32[3,38,3,256]{3,2,1,0:T(4,128)} collective-permute-done((f32[3,38,3,256]{3,2,1,0:T(4,128)}, f32[3,38,3,256]{3,2,1,0:T(4,128)}, u32[]{:S(2)}, u32[]{:S(2)}) %collective-permute-start.18) | collective-permute-done | bytes 350240 | tf_op jit(solution)/shard_map/ppermute | solution.py:26
  355.9 8.2 %collective-permute-done.19 = f32[3,38,3,256]{3,2,1,0:T(4,128)} collective-permute-done((f32[3,38,3,256]{3,2,1,0:T(4,128)S(1)}, f32[3,38,3,256]{3,2,1,0:T(4,128)}, u32[]{:S(2)}, u32[]{:S(2)}) %collective-permute-start.19) | collective-permute-done | bytes 350240 | tf_op jit(solution)/shard_map/ppermute | solution.py:25
  364.1 1.7 pad_maximum_fusion.3
  365.8 2.6 fusion.92
  370.7 1.3 collective-permute-start.20
  372.0 4.5 collective-permute-start.21
  376.9 1.6 collective-permute-done.21
  380.0 4.9 collective-permute-start.23
  385.3 8.6 %collective-permute-done.22 = f32[3,38,3,256]{3,2,1,0:T(4,128)S(1)} collective-permute-done((f32[3,38,3,256]{3,2,1,0:T(4,128)S(1)}, f32[3,38,3,256]{3,2,1,0:T(4,128)S(1)}, u32[]{:S(2)}, u32[]{:S(2)}) %collective-permute-start.22) | collective-permute-done | bytes 350240 | tf_op jit(solution)/shard_map/ppermute | solution.py:26
  394.0 10.2 %collective-permute-done.23 = f32[3,38,3,256]{3,2,1,0:T(4,128)S(1)} collective-permute-done((f32[3,38,3,256]{3,2,1,0:T(4,128)S(1)}, f32[3,38,3,256]{3,2,1,0:T(4,128)S(1)}, u32[]{:S(2)}, u32[]{:S(2)}) %collective-permute-start.23) | collective-permute-done | bytes 350240 | tf_op jit(solution)/shard_map/ppermute | solution.py:25
  404.7 1.6 fusion.76
  408.2 4.5 collective-permute-start.25
  413.1 1.6 collective-permute-done.25
  416.2 5.3 %collective-permute-start.27 = (f32[3,38,3,256]{3,2,1,0:T(4,128)S(1)}, f32[3,38,3,256]{3,2,1,0:T(4,128)S(1)}, u32[]{:S(2)}, u32[]{:S(2)}) collective-permute-start(f32[3,38,3,256]{3,2,1,0:T(4,128)S(1)} %get-tuple-element.324), channel_id=1, source_target_pairs={{0,1},{1,2},{2,3},{3,4},{4,5},{5,6},{6,7},{8,9},{9,10},{10,11},{11... | collective-permute-start | bytes 1050632 | tf_op jit(solution)/shard_map/ppermute | solution.py:25
  422.0 8.9 %collective-permute-done.26 = f32[3,38,3,256]{3,2,1,0:T(4,128)S(1)} collective-permute-done((f32[3,38,3,256]{3,2,1,0:T(4,128)S(1)}, f32[3,38,3,256]{3,2,1,0:T(4,128)S(1)}, u32[]{:S(2)}, u32[]{:S(2)}) %collective-permute-start.26) | collective-permute-done | bytes 350240 | tf_op jit(solution)/shard_map/ppermute | solution.py:26
  430.8 10.2 %collective-permute-done.27 = f32[3,38,3,256]{3,2,1,0:T(4,128)S(1)} collective-permute-done((f32[3,38,3,256]{3,2,1,0:T(4,128)S(1)}, f32[3,38,3,256]{3,2,1,0:T(4,128)S(1)}, u32[]{:S(2)}, u32[]{:S(2)}) %collective-permute-start.27) | collective-permute-done | bytes 350240 | tf_op jit(solution)/shard_map/ppermute | solution.py:25
  441.5 1.6 fusion.60
  444.9 4.5 collective-permute-start.29
  449.9 1.6 collective-permute-done.29
  453.0 5.0 %collective-permute-start.31 = (f32[3,38,3,256]{3,2,1,0:T(4,128)S(1)}, f32[3,38,3,256]{3,2,1,0:T(4,128)S(1)}, u32[]{:S(2)}, u32[]{:S(2)}) collective-permute-start(f32[3,38,3,256]{3,2,1,0:T(4,128)S(1)} %get-tuple-element.320), channel_id=1, source_target_pairs={{0,1},{1,2},{2,3},{3,4},{4,5},{5,6},{6,7},{8,9},{9,10},{10,11},{11... | collective-permute-start | bytes 1050632 | tf_op jit(solution)/shard_map/ppermute | solution.py:25
  458.5 8.6 %collective-permute-done.30 = f32[3,38,3,256]{3,2,1,0:T(4,128)S(1)} collective-permute-done((f32[3,38,3,256]{3,2,1,0:T(4,128)S(1)}, f32[3,38,3,256]{3,2,1,0:T(4,128)S(1)}, u32[]{:S(2)}, u32[]{:S(2)}) %collective-permute-start.30) | collective-permute-done | bytes 350240 | tf_op jit(solution)/shard_map/ppermute | solution.py:26
  467.1 10.2 %collective-permute-done.31 = f32[3,38,3,256]{3,2,1,0:T(4,128)S(1)} collective-permute-done((f32[3,38,3,256]{3,2,1,0:T(4,128)S(1)}, f32[3,38,3,256]{3,2,1,0:T(4,128)S(1)}, u32[]{:S(2)}, u32[]{:S(2)}) %collective-permute-start.31) | collective-permute-done | bytes 350240 | tf_op jit(solution)/shard_map/ppermute | solution.py:25
  477.8 1.6 fusion.44
  479.6 1.5 multiply_add_fusion
  (199 shorter events, 52.7 us)
Async XLA Ops:
  7.2 171.1 %reduce-scatter.3.cloned.1.call-start = ((), (), s32[]{:S(2)}) async-start(), calls=%async_computation.2 | async-start | bytes 655360 | tf_op jit(solution)/shard_map/reduce_scatter | solution.py:133
  8.1 149.7 %collective-permute-start.1 = (f32[3,3,8,256]{3,2,1,0:T(8,128)S(1)}, f32[3,3,8,256]{3,2,1,0:T(8,128)S(1)}, u32[]{:S(2)}, u32[]{:S(2)}) collective-permute-start(f32[3,3,8,256]{3,2,1,0:T(8,128)S(1)} %get-tuple-element.397), channel_id=1, source_target_pairs={{0,8},{8,16},{16,24},{1,9},{9,17},{17,25},{2,10},{10,18},{18,26},{... | collective-permute-start | bytes 221192 | tf_op jit(solution)/shard_map/ppermute | solution.py:25
  13.1 145.1 %collective-permute-start = (f32[3,3,8,256]{3,2,1,0:T(8,128)S(1)}, f32[3,3,8,256]{3,2,1,0:T(8,128)S(1)}, u32[]{:S(2)}, u32[]{:S(2)}) collective-permute-start(f32[3,3,8,256]{3,2,1,0:T(8,128)S(1)} %get-tuple-element.396), channel_id=1, source_target_pairs={{8,0},{16,8},{24,16},{9,1},{17,9},{25,17},{10,2},{18,10},{26,18},{... | collective-permute-start | bytes 221192 | tf_op jit(solution)/shard_map/ppermute | solution.py:26
  15.7 78.0 %copy-start.31 = (pred[256]{0:T(512)(128)(4,1)}, pred[256]{0:T(512)(128)(4,1)S(1)}, u32[]{:S(2)}) copy-start(pred[256]{0:T(512)(128)(4,1)S(1)} %compare_and_fusion) | copy-start | bytes 772
  16.5 77.2 %copy-start.21 = (f32[1,256]{1,0:T(1,128)}, f32[1,256]{1,0:T(1,128)S(1)}, u32[]{:S(2)}) copy-start(f32[1,256]{1,0:T(1,128)S(1)} %get-tuple-element.405) | copy-start | bytes 3076
  16.5 77.2 %copy-start.23 = (f32[1,256]{1,0:T(1,128)}, f32[1,256]{1,0:T(1,128)S(1)}, u32[]{:S(2)}) copy-start(f32[1,256]{1,0:T(1,128)S(1)} %get-tuple-element.406) | copy-start | bytes 3076
  16.5 77.2 %copy-start.25 = (f32[1,256]{1,0:T(1,128)}, f32[1,256]{1,0:T(1,128)S(1)}, u32[]{:S(2)}) copy-start(f32[1,256]{1,0:T(1,128)S(1)} %get-tuple-element.407) | copy-start | bytes 3076
  90.7 3.1 copy-start.27
  93.1 31.7 %copy-start.33 = (f32[256]{0:T(256)S(1)}, f32[256]{0:T(256)}, u32[]{:S(2)}) copy-start(f32[256]{0:T(256)} %param.18) | copy-start | bytes 3076
  156.7 1.4 copy-start.6
  156.7 1.4 copy-start.8
  157.8 210.9 %reduce-scatter.5.cloned.1.call-start = ((), (), s32[]{:S(2)}) async-start(), calls=%async_computation.3 | async-start | bytes 655360 | tf_op jit(solution)/shard_map/reduce_scatter | solution.py:133
  159.1 9.3 %copy-start.5 = (f32[3,38,8,256]{3,2,1,0:T(8,128)}, f32[3,38,8,256]{3,2,1,0:T(8,128)S(1)}, u32[]{:S(2)}) copy-start(f32[3,38,8,256]{3,2,1,0:T(8,128)S(1)} %get-tuple-element.402) | copy-start | bytes 2801668
  160.3 10.7 %collective-permute-start.2 = (f32[3,38,3,256]{3,2,1,0:T(4,128)}, f32[3,38,3,256]{3,2,1,0:T(4,128)S(1)}, u32[]{:S(2)}, u32[]{:S(2)}) collective-permute-start(f32[3,38,3,256]{3,2,1,0:T(4,128)} %get-tuple-element.345), channel_id=1, source_target_pairs={{1,0},{2,1},{3,2},{4,3},{5,4},{6,5},{7,6},{9,8},{10,9},{11,10},{12... | collective-permute-start | bytes 1050632 | tf_op jit(solution)/shard_map/ppermute | solution.py:26
  161.6 6.9 %copy-start.30 = (f32[32,8]{0,1:T(8,128)S(1)}, f32[32,8]{0,1:T(8,128)}, u32[]{:S(2)}) copy-start(f32[32,8]{0,1:T(8,128)} %param.15) | copy-start | bytes 3076
  161.6 10.9 %collective-permute-start.3 = (f32[3,38,3,256]{3,2,1,0:T(4,128)}, f32[3,38,3,256]{3,2,1,0:T(4,128)}, u32[]{:S(2)}, u32[]{:S(2)}) collective-permute-start(f32[3,38,3,256]{3,2,1,0:T(4,128)} %get-tuple-element.346), channel_id=1, source_target_pairs={{0,1},{1,2},{2,3},{3,4},{4,5},{5,6},{6,7},{8,9},{9,10},{10,11},{11... | collective-permute-start | bytes 1050632 | tf_op jit(solution)/shard_map/ppermute | solution.py:25
  170.9 1.6 copy-start.16
  172.5 6.9 %copy-start.17 = (f32[3,256]{1,0:T(4,128)S(1)}, f32[3,256]{1,0:T(4,128)}, u32[]{:S(2)}) copy-start(f32[3,256]{1,0:T(4,128)} %param.17) | copy-start | bytes 9220
  172.5 6.9 %copy-start.19 = (s32[256]{0:T(256)S(1)}, s32[256]{0:T(256)}, u32[]{:S(2)}) copy-start(s32[256]{0:T(256)} %param.19) | copy-start | bytes 3076
  178.3 1.8 copy-start.4
  180.3 6.2 %collective-permute-start.4 = (f32[3,3,8,256]{3,2,1,0:T(8,128)S(1)}, f32[3,3,8,256]{3,2,1,0:T(8,128)S(1)}, u32[]{:S(2)}, u32[]{:S(2)}) collective-permute-start(f32[3,3,8,256]{3,2,1,0:T(8,128)S(1)} %get-tuple-element.387), channel_id=1, source_target_pairs={{8,0},{16,8},{24,16},{9,1},{17,9},{25,17},{10,2},{18,10},{26,18},{... | collective-permute-start | bytes 221192 | tf_op jit(solution)/shard_map/ppermute | solution.py:26
  181.6 6.5 %collective-permute-start.5 = (f32[3,3,8,256]{3,2,1,0:T(8,128)S(1)}, f32[3,3,8,256]{3,2,1,0:T(8,128)S(1)}, u32[]{:S(2)}, u32[]{:S(2)}) collective-permute-start(f32[3,3,8,256]{3,2,1,0:T(8,128)S(1)} %get-tuple-element.388), channel_id=1, source_target_pairs={{0,8},{8,16},{16,24},{1,9},{9,17},{17,25},{2,10},{10,18},{18,26},{... | collective-permute-start | bytes 221192 | tf_op jit(solution)/shard_map/ppermute | solution.py:25
  188.4 15.8 %collective-permute-start.6 = (f32[3,38,3,256]{3,2,1,0:T(4,128)S(1)}, f32[3,38,3,256]{3,2,1,0:T(4,128)S(1)}, u32[]{:S(2)}, u32[]{:S(2)}) collective-permute-start(f32[3,38,3,256]{3,2,1,0:T(4,128)S(1)} %get-tuple-element.343), channel_id=1, source_target_pairs={{1,0},{2,1},{3,2},{4,3},{5,4},{6,5},{7,6},{9,8},{10,9},{11,10},{12... | collective-permute-start | bytes 1050632 | tf_op jit(solution)/shard_map/ppermute | solution.py:26
  189.7 24.7 %collective-permute-start.7 = (f32[3,38,3,256]{3,2,1,0:T(4,128)S(1)}, f32[3,38,3,256]{3,2,1,0:T(4,128)S(1)}, u32[]{:S(2)}, u32[]{:S(2)}) collective-permute-start(f32[3,38,3,256]{3,2,1,0:T(4,128)S(1)} %get-tuple-element.344), channel_id=1, source_target_pairs={{0,1},{1,2},{2,3},{3,4},{4,5},{5,6},{6,7},{8,9},{9,10},{10,11},{11... | collective-permute-start | bytes 1050632 | tf_op jit(solution)/shard_map/ppermute | solution.py:25
  217.1 35.9 %copy-start.1 = (f32[3,32,8,256]{3,2,1,0:T(8,128)}, f32[3,32,8,256]{3,2,1,0:T(8,128)S(1)}, u32[]{:S(2)}) copy-start(f32[3,32,8,256]{3,2,1,0:T(8,128)S(1)} %get-tuple-element.290) | copy-start | bytes 2359300
  217.2 6.2 %collective-permute-start.8 = (f32[3,3,8,256]{3,2,1,0:T(8,128)S(1)}, f32[3,3,8,256]{3,2,1,0:T(8,128)S(1)}, u32[]{:S(2)}, u32[]{:S(2)}) collective-permute-start(f32[3,3,8,256]{3,2,1,0:T(8,128)S(1)} %get-tuple-element.381), channel_id=1, source_target_pairs={{8,0},{16,8},{24,16},{9,1},{17,9},{25,17},{10,2},{18,10},{26,18},{... | collective-permute-start | bytes 221192 | tf_op jit(solution)/shard_map/ppermute | solution.py:26
  218.5 6.5 %collective-permute-start.9 = (f32[3,3,8,256]{3,2,1,0:T(8,128)S(1)}, f32[3,3,8,256]{3,2,1,0:T(8,128)S(1)}, u32[]{:S(2)}, u32[]{:S(2)}) collective-permute-start(f32[3,3,8,256]{3,2,1,0:T(8,128)S(1)} %get-tuple-element.382), channel_id=1, source_target_pairs={{0,8},{8,16},{16,24},{1,9},{9,17},{17,25},{2,10},{10,18},{18,26},{... | collective-permute-start | bytes 221192 | tf_op jit(solution)/shard_map/ppermute | solution.py:25
  225.2 15.4 %collective-permute-start.10 = (f32[3,38,3,256]{3,2,1,0:T(4,128)S(1)}, f32[3,38,3,256]{3,2,1,0:T(4,128)S(1)}, u32[]{:S(2)}, u32[]{:S(2)}) collective-permute-start(f32[3,38,3,256]{3,2,1,0:T(4,128)S(1)} %get-tuple-element.339), channel_id=1, source_target_pairs={{1,0},{2,1},{3,2},{4,3},{5,4},{6,5},{7,6},{9,8},{10,9},{11,10},{12... | collective-permute-start | bytes 1050632 | tf_op jit(solution)/shard_map/ppermute | solution.py:26
  226.5 24.3 %collective-permute-start.11 = (f32[3,38,3,256]{3,2,1,0:T(4,128)S(1)}, f32[3,38,3,256]{3,2,1,0:T(4,128)S(1)}, u32[]{:S(2)}, u32[]{:S(2)}) collective-permute-start(f32[3,38,3,256]{3,2,1,0:T(4,128)S(1)} %get-tuple-element.340), channel_id=1, source_target_pairs={{0,1},{1,2},{2,3},{3,4},{4,5},{5,6},{6,7},{8,9},{9,10},{10,11},{11... | collective-permute-start | bytes 1050632 | tf_op jit(solution)/shard_map/ppermute | solution.py:25
  253.3 6.2 %collective-permute-start.12 = (f32[3,3,8,256]{3,2,1,0:T(8,128)S(1)}, f32[3,3,8,256]{3,2,1,0:T(8,128)S(1)}, u32[]{:S(2)}, u32[]{:S(2)}) collective-permute-start(f32[3,3,8,256]{3,2,1,0:T(8,128)S(1)} %get-tuple-element.375), channel_id=1, source_target_pairs={{8,0},{16,8},{24,16},{9,1},{17,9},{25,17},{10,2},{18,10},{26,18},{... | collective-permute-start | bytes 221192 | tf_op jit(solution)/shard_map/ppermute | solution.py:26
  254.6 6.5 %collective-permute-start.13 = (f32[3,3,8,256]{3,2,1,0:T(8,128)S(1)}, f32[3,3,8,256]{3,2,1,0:T(8,128)S(1)}, u32[]{:S(2)}, u32[]{:S(2)}) collective-permute-start(f32[3,3,8,256]{3,2,1,0:T(8,128)S(1)} %get-tuple-element.376), channel_id=1, source_target_pairs={{0,8},{8,16},{16,24},{1,9},{9,17},{17,25},{2,10},{10,18},{18,26},{... | collective-permute-start | bytes 221192 | tf_op jit(solution)/shard_map/ppermute | solution.py:25
  259.6 1.8 copy-start.11
  261.8 15.9 %collective-permute-start.14 = (f32[3,38,3,256]{3,2,1,0:T(4,128)S(1)}, f32[3,38,3,256]{3,2,1,0:T(4,128)S(1)}, u32[]{:S(2)}, u32[]{:S(2)}) collective-permute-start(f32[3,38,3,256]{3,2,1,0:T(4,128)S(1)} %get-tuple-element.335), channel_id=1, source_target_pairs={{1,0},{2,1},{3,2},{4,3},{5,4},{6,5},{7,6},{9,8},{10,9},{11,10},{12... | collective-permute-start | bytes 1050632 | tf_op jit(solution)/shard_map/ppermute | solution.py:26
  263.1 24.8 %collective-permute-start.15 = (f32[3,38,3,256]{3,2,1,0:T(4,128)S(1)}, f32[3,38,3,256]{3,2,1,0:T(4,128)S(1)}, u32[]{:S(2)}, u32[]{:S(2)}) collective-permute-start(f32[3,38,3,256]{3,2,1,0:T(4,128)S(1)} %get-tuple-element.336), channel_id=1, source_target_pairs={{0,1},{1,2},{2,3},{3,4},{4,5},{5,6},{6,7},{8,9},{9,10},{10,11},{11... | collective-permute-start | bytes 1050632 | tf_op jit(solution)/shard_map/ppermute | solution.py:25
  268.3 19.6 %copy-start.12 = (f32[3,3,8,256]{3,2,1,0:T(8,128)S(1)}, f32[3,3,8,256]{3,2,1,0:T(8,128)}, u32[]{:S(2)}) copy-start(f32[3,3,8,256]{3,2,1,0:T(8,128)} %copy-done.11) | copy-start | bytes 221188
  268.3 19.6 %copy-start.14 = (f32[3,3,8,256]{3,2,1,0:T(8,128)S(1)}, f32[3,3,8,256]{3,2,1,0:T(8,128)}, u32[]{:S(2)}) copy-start(f32[3,3,8,256]{3,2,1,0:T(8,128)} %copy-done.13) | copy-start | bytes 221188
  288.4 1.8 copy-start.2
  290.6 1.8 copy-start.32
  290.6 1.9 copy-start.22
  290.6 1.9 copy-start.24
  290.6 1.9 copy-start.26
  291.1 39.3 %copy-start.7 = (f32[3,2048]{1,0:T(4,128)S(1)}, f32[3,2048]{1,0:T(4,128)}, u32[]{:S(2)}) copy-start(f32[3,2048]{1,0:T(4,128)} %copy-done.6) | copy-start | bytes 73732
  291.1 39.3 %copy-start.9 = (f32[3,2048]{1,0:T(4,128)S(1)}, f32[3,2048]{1,0:T(4,128)}, u32[]{:S(2)}) copy-start(f32[3,2048]{1,0:T(4,128)} %copy-done.8) | copy-start | bytes 73732
  291.1 39.3 %copy-start.29 = (f32[2048]{0:T(1024)S(1)}, f32[2048]{0:T(1024)}, u32[]{:S(2)}) copy-start(f32[2048]{0:T(1024)} %copy-done.28) | copy-start | bytes 24580
  324.2 17.5 %collective-permute-start.16 = (f32[3,3,8,256]{3,2,1,0:T(8,128)S(1)}, f32[3,3,8,256]{3,2,1,0:T(8,128)S(1)}, u32[]{:S(2)}, u32[]{:S(2)}) collective-permute-start(f32[3,3,8,256]{3,2,1,0:T(8,128)S(1)} %get-tuple-element.369), channel_id=1, source_target_pairs={{8,0},{16,8},{24,16},{9,1},{17,9},{25,17},{10,2},{18,10},{26,18},{... | collective-permute-start | bytes 221192 | tf_op jit(solution)/shard_map/ppermute | solution.py:26
  325.5 16.2 %collective-permute-start.17 = (f32[3,3,8,256]{3,2,1,0:T(8,128)S(1)}, f32[3,3,8,256]{3,2,1,0:T(8,128)S(1)}, u32[]{:S(2)}, u32[]{:S(2)}) collective-permute-start(f32[3,3,8,256]{3,2,1,0:T(8,128)S(1)} %get-tuple-element.370), channel_id=1, source_target_pairs={{0,8},{8,16},{16,24},{1,9},{9,17},{17,25},{2,10},{10,18},{18,26},{... | collective-permute-start | bytes 221192 | tf_op jit(solution)/shard_map/ppermute | solution.py:25
  341.7 22.3 %copy-start.10 = (f32[3,3,8,256]{3,2,1,0:T(8,128)}, f32[3,3,8,256]{3,2,1,0:T(8,128)S(1)}, u32[]{:S(2)}) copy-start(f32[3,3,8,256]{3,2,1,0:T(8,128)S(1)} %collective-permute-done.17) | copy-start | bytes 221188
  342.7 13.1 %collective-permute-start.18 = (f32[3,38,3,256]{3,2,1,0:T(4,128)}, f32[3,38,3,256]{3,2,1,0:T(4,128)}, u32[]{:S(2)}, u32[]{:S(2)}) collective-permute-start(f32[3,38,3,256]{3,2,1,0:T(4,128)} %get-tuple-element.331), channel_id=1, source_target_pairs={{1,0},{2,1},{3,2},{4,3},{5,4},{6,5},{7,6},{9,8},{10,9},{11,10},{12... | collective-permute-start | bytes 1050632 | tf_op jit(solution)/shard_map/ppermute | solution.py:26
  344.0 20.0 %collective-permute-start.19 = (f32[3,38,3,256]{3,2,1,0:T(4,128)S(1)}, f32[3,38,3,256]{3,2,1,0:T(4,128)}, u32[]{:S(2)}, u32[]{:S(2)}) collective-permute-start(f32[3,38,3,256]{3,2,1,0:T(4,128)S(1)} %get-tuple-element.332), channel_id=1, source_target_pairs={{0,1},{1,2},{2,3},{3,4},{4,5},{5,6},{6,7},{8,9},{9,10},{10,11},{11... | collective-permute-start | bytes 1050632 | tf_op jit(solution)/shard_map/ppermute | solution.py:25
  365.8 2.9 copy-start.15
  365.8 3.9 copy-start.18
  365.8 3.9 copy-start.20
  370.7 6.2 %collective-permute-start.20 = (f32[3,3,8,256]{3,2,1,0:T(8,128)S(1)}, f32[3,3,8,256]{3,2,1,0:T(8,128)S(1)}, u32[]{:S(2)}, u32[]{:S(2)}) collective-permute-start(f32[3,3,8,256]{3,2,1,0:T(8,128)S(1)} %get-tuple-element.363), channel_id=1, source_target_pairs={{8,0},{16,8},{24,16},{9,1},{17,9},{25,17},{10,2},{18,10},{26,18},{... | collective-permute-start | bytes 221192 | tf_op jit(solution)/shard_map/ppermute | solution.py:26
  372.0 6.5 %collective-permute-start.21 = (f32[3,3,8,256]{3,2,1,0:T(8,128)S(1)}, f32[3,3,8,256]{3,2,1,0:T(8,128)S(1)}, u32[]{:S(2)}, u32[]{:S(2)}) collective-permute-start(f32[3,3,8,256]{3,2,1,0:T(8,128)S(1)} %get-tuple-element.364), channel_id=1, source_target_pairs={{0,8},{8,16},{16,24},{1,9},{9,17},{17,25},{2,10},{10,18},{18,26},{... | collective-permute-start | bytes 221192 | tf_op jit(solution)/shard_map/ppermute | solution.py:25
  378.7 15.2 %collective-permute-start.22 = (f32[3,38,3,256]{3,2,1,0:T(4,128)S(1)}, f32[3,38,3,256]{3,2,1,0:T(4,128)S(1)}, u32[]{:S(2)}, u32[]{:S(2)}) collective-permute-start(f32[3,38,3,256]{3,2,1,0:T(4,128)S(1)} %get-tuple-element.327), channel_id=1, source_target_pairs={{1,0},{2,1},{3,2},{4,3},{5,4},{6,5},{7,6},{9,8},{10,9},{11,10},{12... | collective-permute-start | bytes 1050632 | tf_op jit(solution)/shard_map/ppermute | solution.py:26
  380.0 24.1 %collective-permute-start.23 = (f32[3,38,3,256]{3,2,1,0:T(4,128)S(1)}, f32[3,38,3,256]{3,2,1,0:T(4,128)S(1)}, u32[]{:S(2)}, u32[]{:S(2)}) collective-permute-start(f32[3,38,3,256]{3,2,1,0:T(4,128)S(1)} %get-tuple-element.328), channel_id=1, source_target_pairs={{0,1},{1,2},{2,3},{3,4},{4,5},{5,6},{6,7},{8,9},{9,10},{10,11},{11... | collective-permute-start | bytes 1050632 | tf_op jit(solution)/shard_map/ppermute | solution.py:25
  406.9 6.2 %collective-permute-start.24 = (f32[3,3,8,256]{3,2,1,0:T(8,128)S(1)}, f32[3,3,8,256]{3,2,1,0:T(8,128)S(1)}, u32[]{:S(2)}, u32[]{:S(2)}) collective-permute-start(f32[3,3,8,256]{3,2,1,0:T(8,128)S(1)} %get-tuple-element.357), channel_id=1, source_target_pairs={{8,0},{16,8},{24,16},{9,1},{17,9},{25,17},{10,2},{18,10},{26,18},{... | collective-permute-start | bytes 221192 | tf_op jit(solution)/shard_map/ppermute | solution.py:26
  408.2 6.5 %collective-permute-start.25 = (f32[3,3,8,256]{3,2,1,0:T(8,128)S(1)}, f32[3,3,8,256]{3,2,1,0:T(8,128)S(1)}, u32[]{:S(2)}, u32[]{:S(2)}) collective-permute-start(f32[3,3,8,256]{3,2,1,0:T(8,128)S(1)} %get-tuple-element.358), channel_id=1, source_target_pairs={{0,8},{8,16},{16,24},{1,9},{9,17},{17,25},{2,10},{10,18},{18,26},{... | collective-permute-start | bytes 221192 | tf_op jit(solution)/shard_map/ppermute | solution.py:25
  414.9 15.9 %collective-permute-start.26 = (f32[3,38,3,256]{3,2,1,0:T(4,128)S(1)}, f32[3,38,3,256]{3,2,1,0:T(4,128)S(1)}, u32[]{:S(2)}, u32[]{:S(2)}) collective-permute-start(f32[3,38,3,256]{3,2,1,0:T(4,128)S(1)} %get-tuple-element.323), channel_id=1, source_target_pairs={{1,0},{2,1},{3,2},{4,3},{5,4},{6,5},{7,6},{9,8},{10,9},{11,10},{12... | collective-permute-start | bytes 1050632 | tf_op jit(solution)/shard_map/ppermute | solution.py:26
  416.2 24.8 %collective-permute-start.27 = (f32[3,38,3,256]{3,2,1,0:T(4,128)S(1)}, f32[3,38,3,256]{3,2,1,0:T(4,128)S(1)}, u32[]{:S(2)}, u32[]{:S(2)}) collective-permute-start(f32[3,38,3,256]{3,2,1,0:T(4,128)S(1)} %get-tuple-element.324), channel_id=1, source_target_pairs={{0,1},{1,2},{2,3},{3,4},{4,5},{5,6},{6,7},{8,9},{9,10},{10,11},{11... | collective-permute-start | bytes 1050632 | tf_op jit(solution)/shard_map/ppermute | solution.py:25
  443.6 6.2 %collective-permute-start.28 = (f32[3,3,8,256]{3,2,1,0:T(8,128)S(1)}, f32[3,3,8,256]{3,2,1,0:T(8,128)S(1)}, u32[]{:S(2)}, u32[]{:S(2)}) collective-permute-start(f32[3,3,8,256]{3,2,1,0:T(8,128)S(1)} %get-tuple-element.351), channel_id=1, source_target_pairs={{8,0},{16,8},{24,16},{9,1},{17,9},{25,17},{10,2},{18,10},{26,18},{... | collective-permute-start | bytes 221192 | tf_op jit(solution)/shard_map/ppermute | solution.py:26
  444.9 6.5 %collective-permute-start.29 = (f32[3,3,8,256]{3,2,1,0:T(8,128)S(1)}, f32[3,3,8,256]{3,2,1,0:T(8,128)S(1)}, u32[]{:S(2)}, u32[]{:S(2)}) collective-permute-start(f32[3,3,8,256]{3,2,1,0:T(8,128)S(1)} %get-tuple-element.352), channel_id=1, source_target_pairs={{0,8},{8,16},{16,24},{1,9},{9,17},{17,25},{2,10},{10,18},{18,26},{... | collective-permute-start | bytes 221192 | tf_op jit(solution)/shard_map/ppermute | solution.py:25
  451.7 15.4 %collective-permute-start.30 = (f32[3,38,3,256]{3,2,1,0:T(4,128)S(1)}, f32[3,38,3,256]{3,2,1,0:T(4,128)S(1)}, u32[]{:S(2)}, u32[]{:S(2)}) collective-permute-start(f32[3,38,3,256]{3,2,1,0:T(4,128)S(1)} %get-tuple-element.319), channel_id=1, source_target_pairs={{1,0},{2,1},{3,2},{4,3},{5,4},{6,5},{7,6},{9,8},{10,9},{11,10},{12... | collective-permute-start | bytes 1050632 | tf_op jit(solution)/shard_map/ppermute | solution.py:26
  453.0 24.3 %collective-permute-start.31 = (f32[3,38,3,256]{3,2,1,0:T(4,128)S(1)}, f32[3,38,3,256]{3,2,1,0:T(4,128)S(1)}, u32[]{:S(2)}, u32[]{:S(2)}) collective-permute-start(f32[3,38,3,256]{3,2,1,0:T(4,128)S(1)} %get-tuple-element.320), channel_id=1, source_target_pairs={{0,1},{1,2},{2,3},{3,4},{4,5},{5,6},{6,7},{8,9},{9,10},{10,11},{11... | collective-permute-start | bytes 1050632 | tf_op jit(solution)/shard_map/ppermute | solution.py:25
  (4 other events, 4.1 us)
Sparse Core Ops, SparseCore 0:
  157.9 18.1 reduce-scatter.2
  350.7 17.9 reduce-scatter.4
